TPU v7x, 256 devices: a whole 4x4x8 slice. The times are simulated.
256 devices in a mesh: slab: 8 (over y, core), grp: 32 (over x, z).
Axes of the slice: x: 4, y: 4, z: 8, core: 2. Of those that a mesh axis runs over, the one named last changes fastest.
Arguments:
- diag_jac: bfloat16 [3072, 625, 625], P(('slab', 'grp')), may hold values from -0.75 to 0.75
- xface_jac: bfloat16 [3072, 2, 15625], P(('slab', 'grp')), may hold values from -1.5 to 1.5
- side_jac: bfloat16 [3072, 4, 15625], P(('slab', 'grp')), may hold values from -1.5 to 1.5
- orient: int32 [3072], P(('slab', 'grp')), may hold values from 0 to 3
- owner: int32 [3072], P(('slab', 'grp')), may hold values from 0 to 7, as said below
Outputs:
- agglomerated: bfloat16 [16384, 7, 1600], P(('slab', 'grp'))
Inputs may be any that keep to these rules, and one draw needn't show every extreme that they name: An element's owner is a grp index below 8 on its own slab. Among the 12 elements of one device at most 2 share an owner; on every slab one owner receives exactly 2 elements from every device of that slab.
All inputs are finite; a program needn't handle non-finite values.
Results may differ from a plain program's by a relative error of at most 0.001.
Values may be sent and summed in bfloat16 or wider, within the bound.
A program may use at most 64 MiB of HBM per device.

v0:
```python
import jax
import jax.numpy as jnp
import numpy as np
from jax import lax
from jax.sharding import PartitionSpec as P

NV = 5
PF = 4
PM = 2
PC = 1


def shifted(array, axis, by):
    devices = lax.axis_size(axis)
    return lax.ppermute(array, axis, [(i, (i + by) % devices) for i in range(devices)])


def gll_points(degree):
    if degree == 1:
        return np.array([-1.0, 1.0])
    if degree == 2:
        return np.array([-1.0, 0.0, 1.0])
    inner_pt = np.sqrt(3.0 / 7.0)
    return np.array([-1.0, -inner_pt, 0.0, inner_pt, 1.0])


def lagrange(source_deg, target_deg):
    source = gll_points(source_deg)
    target = gll_points(target_deg)
    result = np.ones((target_deg + 1, source_deg + 1))
    for j in range(source_deg + 1):
        for m in range(source_deg + 1):
            if m != j:
                result[:, j] = result[:, j] * (target - source[m]) / (source[j] - source[m])
    return result


def grid_coords(nvars, side, dims):
    flat = np.arange(nvars * side**dims)
    parts = []
    for power in range(dims, -1, -1):
        parts.append(flat // side**power % (side if power < dims else nvars))
    return parts


def turn_table(nvars, side, with_x):
    if with_x:
        coords = grid_coords(nvars, side, 3)
        first, second = (coords[2], coords[3])
    else:
        coords = grid_coords(nvars, side, 2)
        first, second = (coords[1], coords[2])
    tables = []
    for turns in range(4):
        if with_x:
            index = ((coords[0] * side + coords[1]) * side + first) * side + second
        else:
            index = (coords[0] * side + first) * side + second
        tables.append(index)
        first, second = (side - 1 - second, first)
    return np.stack(tables).astype(np.int32)


def build_tables(nvars, fine_deg, mid_deg, coarse_deg):
    fine_mid = lagrange(mid_deg, fine_deg)
    mid_coarse = lagrange(coarse_deg, mid_deg)

    def cube(line):
        return np.kron(np.eye(nvars), np.kron(np.kron(line, line), line))

    upper = cube(fine_mid)
    lower = cube(mid_coarse)
    count = fine_deg + 1
    coords = grid_coords(nvars, count, 3)
    faces = []
    for axis_num in (1, 2, 3):
        for level in (0, fine_deg):
            faces.append(upper[coords[axis_num] == level])
    face_rows = np.stack(faces)
    coarse_turns = turn_table(nvars, coarse_deg + 1, True)
    face_turns = turn_table(nvars, count, False)
    return (
        upper.astype(np.float32),
        lower.astype(np.float32),
        face_rows.astype(np.float32),
        coarse_turns,
        face_turns,
    )


def split_product(blocks, table):
    leading = table.astype(jnp.bfloat16)
    remainder = (table - leading.astype(jnp.float32)).astype(jnp.bfloat16)
    first = jnp.einsum("efab,fbm->efam", blocks, leading, preferred_element_type=jnp.float32)
    second = jnp.einsum("efab,fbm->efam", blocks, remainder, preferred_element_type=jnp.float32)
    return first + second


def shards(diag_jac, xface_jac, side_jac, orient, owner):
    high = lax.Precision.HIGHEST
    upper, lower, face_rows, coarse_turns, face_turns = build_tables(NV, PF, PM, PC)
    upper = jnp.asarray(upper)
    lower = jnp.asarray(lower)
    face_rows = jnp.asarray(face_rows)
    coarse_turns = jnp.asarray(coarse_turns)
    face_turns = jnp.asarray(face_turns)
    elems = diag_jac.shape[0]
    nface = face_rows.shape[1]
    ncoarse = lower.shape[1]
    xface = xface_jac.reshape(elems, 2, nface, nface)
    side = side_jac.reshape(elems, 4, nface, nface)
    picker = (orient[:, None] == jnp.arange(4, dtype=jnp.int32)[None, :]).astype(jnp.int32)
    coarse_perm = jnp.sum(picker[:, :, None] * coarse_turns[None], axis=1)

    def galerkin(blocks, left, right):
        left_c = jnp.einsum("fan,nc->fac", left, lower, precision=high)
        right_c = jnp.einsum("fbm,md->fbd", right, lower, precision=high)
        inner = split_product(blocks, right_c)
        return jnp.einsum("fac,efad->efcd", left_c, inner, precision=high)

    stored = xface[:, 1]
    sent = galerkin(stored[:, None], face_rows[0:1], face_rows[1:2])[:, 0]
    sent = jnp.take_along_axis(sent, coarse_perm[:, :, None], axis=1).astype(jnp.bfloat16)
    minus_c = shifted(sent, "slab", 1).astype(jnp.float32)
    diag_c = galerkin(diag_jac[:, None], upper[None], upper[None])[:, 0]
    plus_c = galerkin(xface[:, 0:1], face_rows[1:2], face_rows[0:1])[:, 0]
    plus_c = jnp.take_along_axis(plus_c, coarse_perm[:, None, :], axis=2)
    side_left = jnp.stack([face_rows[2], face_rows[3], face_rows[4], face_rows[5]])
    side_right = jnp.stack([face_rows[3], face_rows[2], face_rows[5], face_rows[4]])
    side_c = galerkin(side, side_left, side_right)
    rows = jnp.concatenate([diag_c[:, None], minus_c[:, None], plus_c[:, None], side_c], axis=1)
    rows = rows.astype(jnp.bfloat16).reshape(elems, 7, ncoarse * ncoarse)
    grp_size = lax.axis_size("grp")
    owners_n = grp_size // 4
    most = max(2, 3 * elems // (2 * owners_n))
    earlier = jnp.arange(elems)[None, :] < jnp.arange(elems)[:, None]
    same = owner[:, None] == owner[None, :]
    rank = jnp.sum((same & earlier).astype(jnp.int32), axis=1)
    dest = owner * most + rank
    width = ncoarse * ncoarse
    placer = (jnp.arange(grp_size * most, dtype=jnp.int32)[:, None] == dest[None, :]).astype(
        jnp.bfloat16
    )
    packed = jnp.einsum("se,ekc->skc", placer, rows, preferred_element_type=jnp.float32)
    packed = packed.astype(jnp.bfloat16).reshape(grp_size, most, 7, width)
    arrived_rows = lax.all_to_all(packed, "grp", split_axis=0, concat_axis=0, tiled=True)
    return arrived_rows.reshape(grp_size * most, 7, width)


def solution(mesh):
    in_specs = (
        P(("slab", "grp"), None, None),
        P(("slab", "grp"), None, None),
        P(("slab", "grp"), None, None),
        P(("slab", "grp")),
        P(("slab", "grp")),
    )
    out_specs = P(("slab", "grp"), None, None)
    return jax.shard_map(shards, mesh=mesh, in_specs=in_specs, out_specs=out_specs, check_vma=False)
```

profile of v0, /device:TPU:1, one launch (start us, length us, event | category | flops | bytes accessed | tf_op | source)
XLA Modules:
  0.0 95.9 jit_solution(806126683010625744)
XLA Ops:
  0.0 0.8 fusion.31
  0.8 0.8 multiply_reduce_fusion
  1.7 4.7 %reshape.179 = bf16[12,2,125,125]{3,2,1,0:T(8,128)(2,1)S(1)} reshape(bf16[12,2,15625]{2,1,0:T(2,128)(2,1)} %param.10) | data formatting | bytes 1500000 | tf_op jit(solution)/shard_map/reshape | solution.py:110
  6.3 0.2 fusion.22
  6.6 0.2 fusion.12
  6.9 0.3 convolution_bitcast_fusion.1
  7.4 5.0 %gather_fusion = bf16[480,40]{1,0:T(8,128)(2,1)S(1)} fusion(bf16[12,40,40]{2,1,0:T(8,128)(2,1)S(1)} %copy.51, s32[480]{0:T(512)S(1)} %reshape.188), kind=kCustom, calls=%fused_computation | custom fusion | bytes 80640 | tf_op jit(solution)/shard_map/jit(take_along_axis)/gather | solution.py:123
  12.5 0.2 fusion.23
  12.7 0.2 fusion.13
  13.0 0.3 convolution_bitcast_fusion
  13.3 5.0 %gather_fusion.1 = bf16[480,40]{1,0:T(8,128)(2,1)S(1)} fusion(bf16[12,40,40]{1,2,0:T(8,128)(2,1)S(1)} %convolution_bitcast_fusion, s32[480]{0:T(512)S(1)} %reshape.188), kind=kCustom, calls=%fused_computation.1 | custom fusion | bytes 80640 | tf_op jit(solution)/shard_map/jit(take_along_axis)/gather | solution.py:127
  18.5 2.7 %collective-permute-start = (bf16[12,40,40]{1,2,0:T(8,128)(2,1)S(1)}, bf16[12,40,40]{1,2,0:T(8,128)(2,1)S(1)}, u32[]{:S(2)}, u32[]{:S(2)}) collective-permute-start(bf16[12,40,40]{1,2,0:T(8,128)(2,1)S(1)} %get-tuple-element.5), channel_id=1, source_target_pairs={{0,32},{32,64},{64,96},{96,128},{128,160},{160,192},{192,224},{224... | collective-permute-start | bytes 115208 | tf_op jit(solution)/shard_map/ppermute | solution.py:15
  21.2 0.2 convert_reduce_fusion
  21.4 5.9 %reshape.185 = bf16[12,4,125,125]{3,2,1,0:T(8,128)(2,1)S(1)} reshape(bf16[12,4,15625]{2,1,0:T(4,128)(2,1)S(1)} %copy-done.1) | data formatting | bytes 3000000 | tf_op jit(solution)/shard_map/reshape | solution.py:111
  27.3 6.7 %fusion.34 = f32[40,12,625]{2,0,1:T(8,128)S(1)} fusion(bf16[625,40,1]{0,1,2:T(8,128)(2,1)S(1)} %copy-done.5, bf16[12,625,625]{2,1,0:T(8,128)(2,1)} %param.9), kind=kOutput, calls=%fused_computation.52 | convolution fusion | flops 375000000 | bytes 10625000 | tf_op jit(solution)/shard_map/efab,fbm->efam/dot_general | solution.py:94
  34.1 2.8 %fusion = f32[12,625,40]{1,2,0:T(8,128)S(1)} fusion(f32[40,12,625]{2,0,1:T(8,128)S(1)} %fusion.34, bf16[625,40,1]{0,1,2:T(8,128)(2,1)S(1)} %copy-done.4, bf16[12,625,625]{2,1,0:T(8,128)(2,1)S(1)} %copy-done), kind=kOutput, calls=%fused_computation.4 | convolution fusion | flops 375300000 | bytes 11825000 | tf_op jit(solution)/shard_map/efab,fbm->efam/dot_general | solution.py:95
  36.9 0.6 fusion.1
  37.5 0.1 copy-done.6
  37.7 0.6 fusion.8
  38.3 0.2 copy-done.3
  38.6 1.0 %fusion.11 = bf16[12,4,40,40]{2,3,0,1:T(8,128)(2,1)S(1)} fusion(f32[12,4,125,40]{2,3,0,1:T(8,128)S(1)} %fusion.8, f32[4,125,40,1]{1,2,3,0:T(8,128)S(1)} %copy-done.3), kind=kOutput, calls=%fused_computation.12 | convolution fusion | flops 115276800 | bytes 1193600 | tf_op jit(solution)/shard_map/fac,efad->efcd/dot_general | solution.py:119
  39.6 1.1 %fusion.14 = bf16[12,1,40,40]{2,3,0,1:T(8,128)(2,1)S(1)} fusion(f32[12,625,40]{1,2,0:T(8,128)S(1)} %fusion, f32[625,40,1]{0,1,2:T(8,128)S(1)} %copy-done.2), kind=kOutput, calls=%fused_computation.20 | convolution fusion | flops 144019200 | bytes 1338400 | tf_op jit(solution)/shard_map/fac,efad->efcd/dot_general | solution.py:119
  41.0 0.1 concatenate.11
  41.1 0.3 copy.65
  41.4 0.4 reshape.213
  41.9 0.1 concatenate.12
  42.1 0.7 convolution_convert_fusion
  42.7 0.6 reshape.186
  43.4 1.0 %copy.60 = bf16[32,2,7,1600]{3,1,2,0:T(2,128)(2,1)S(1)} copy(bf16[32,2,7,1600]{3,1,0,2:T(2,128)(2,1)S(1)} %reshape.186) | data formatting | bytes 2867200 | tf_op jit(solution)/shard_map/reshape | solution.py:145
  44.4 48.4 %all_to_all.5 = bf16[32,2,7,1600]{3,1,2,0:T(2,128)(2,1)S(1)} all-to-all(bf16[32,2,7,1600]{3,1,2,0:T(2,128)(2,1)S(1)} %copy.60), channel_id=1, replica_groups=mesh['slab'=8,'grp'=32] {'grp'}, dimensions={0} | all-to-all | bytes 2867200 | tf_op jit(solution)/shard_map/all_to_all | solution.py:146
  92.8 1.0 %copy.61 = bf16[32,2,7,1600]{3,1,0,2:T(2,128)(2,1)S(1)} copy(bf16[32,2,7,1600]{3,1,2,0:T(2,128)(2,1)S(1)} %all_to_all.5) | data formatting | bytes 2867200 | tf_op jit(solution)/shard_map/all_to_all | solution.py:146
  93.9 2.0 %reshape.187 = bf16[64,7,1600]{2,0,1:T(8,128)(2,1)} reshape(bf16[32,2,7,1600]{3,1,0,2:T(2,128)(2,1)S(1)} %copy.61) | data formatting | bytes 2867200 | tf_op jit(solution)/shard_map/reshape | solution.py:147
  (40 shorter events, 1.0 us)
Async XLA Ops:
  0.0 6.3 %copy-start.13 = (bf16[125,40,1]{0,1,2:T(8,128)(2,1)S(1)}, bf16[125,40,1]{0,1,2:T(8,128)(2,1)}, u32[]{:S(2)}) copy-start(bf16[125,40,1]{0,1,2:T(8,128)(2,1)} %constant.106) | copy-start | bytes 30004
  0.0 6.6 %copy-start.11 = (bf16[125,40,1]{0,1,2:T(8,128)(2,1)S(1)}, bf16[125,40,1]{0,1,2:T(8,128)(2,1)}, u32[]{:S(2)}) copy-start(bf16[125,40,1]{0,1,2:T(8,128)(2,1)} %constant.107) | copy-start | bytes 30004
  0.8 6.1 %copy-start.9 = (f32[125,40,1]{0,1,2:T(8,128)S(1)}, f32[125,40,1]{0,1,2:T(8,128)}, u32[]{:S(2)}) copy-start(f32[125,40,1]{0,1,2:T(8,128)} %constant.108) | copy-start | bytes 60004
  6.6 5.9 %copy-start.12 = (bf16[125,40,1]{0,1,2:T(8,128)(2,1)S(1)}, bf16[125,40,1]{0,1,2:T(8,128)(2,1)}, u32[]{:S(2)}) copy-start(bf16[125,40,1]{0,1,2:T(8,128)(2,1)} %constant.109) | copy-start | bytes 30004
  6.9 5.8 %copy-start.10 = (bf16[125,40,1]{0,1,2:T(8,128)(2,1)S(1)}, bf16[125,40,1]{0,1,2:T(8,128)(2,1)}, u32[]{:S(2)}) copy-start(bf16[125,40,1]{0,1,2:T(8,128)(2,1)} %constant.110) | copy-start | bytes 30004
  7.3 5.6 %copy-start.8 = (f32[125,40,1]{0,1,2:T(8,128)S(1)}, f32[125,40,1]{0,1,2:T(8,128)}, u32[]{:S(2)}) copy-start(f32[125,40,1]{0,1,2:T(8,128)} %constant.111) | copy-start | bytes 60004
  12.7 8.5 %copy-start.14 = (s32[12]{0:T(128)S(1)}, s32[12]{0:T(128)}, u32[]{:S(2)}) copy-start(s32[12]{0:T(128)} %param.13) | copy-start | bytes 148
  12.7 8.7 %copy-start.1 = (bf16[12,4,15625]{2,1,0:T(4,128)(2,1)S(1)}, bf16[12,4,15625]{2,1,0:T(4,128)(2,1)}, u32[]{:S(2)}) copy-start(bf16[12,4,15625]{2,1,0:T(4,128)(2,1)} %param.11) | copy-start | bytes 4500004
  18.5 8.8 %copy-start.5 = (bf16[625,40,1]{0,1,2:T(8,128)(2,1)S(1)}, bf16[625,40,1]{0,1,2:T(8,128)(2,1)}, u32[]{:S(2)}) copy-start(bf16[625,40,1]{0,1,2:T(8,128)(2,1)} %constant.103) | copy-start | bytes 150004
  18.5 23.3 %collective-permute-start = (bf16[12,40,40]{1,2,0:T(8,128)(2,1)S(1)}, bf16[12,40,40]{1,2,0:T(8,128)(2,1)S(1)}, u32[]{:S(2)}, u32[]{:S(2)}) collective-permute-start(bf16[12,40,40]{1,2,0:T(8,128)(2,1)S(1)} %get-tuple-element.5), channel_id=1, source_target_pairs={{0,32},{32,64},{64,96},{96,128},{128,160},{160,192},{192,224},{224... | collective-permute-start | bytes 115208 | tf_op jit(solution)/shard_map/ppermute | solution.py:15
  27.3 6.7 %copy-start = (bf16[12,625,625]{2,1,0:T(8,128)(2,1)S(1)}, bf16[12,625,625]{2,1,0:T(8,128)(2,1)}, u32[]{:S(2)}) copy-start(bf16[12,625,625]{2,1,0:T(8,128)(2,1)} %param.9) | copy-start | bytes 28125004
  27.3 6.7 %copy-start.4 = (bf16[625,40,1]{0,1,2:T(8,128)(2,1)S(1)}, bf16[625,40,1]{0,1,2:T(8,128)(2,1)}, u32[]{:S(2)}) copy-start(bf16[625,40,1]{0,1,2:T(8,128)(2,1)} %constant.104) | copy-start | bytes 150004
  34.1 2.8 %copy-start.7 = (bf16[4,125,40,1]{1,2,3,0:T(8,128)(2,1)S(1)}, bf16[4,125,40,1]{1,2,3,0:T(8,128)(2,1)}, u32[]{:S(2)}) copy-start(bf16[4,125,40,1]{1,2,3,0:T(8,128)(2,1)} %constant.113) | copy-start | bytes 120004
  36.9 0.8 copy-start.6
  37.7 0.9 copy-start.3
  38.6 1.0 %copy-start.2 = (f32[625,40,1]{0,1,2:T(8,128)S(1)}, f32[625,40,1]{0,1,2:T(8,128)}, u32[]{:S(2)}) copy-start(f32[625,40,1]{0,1,2:T(8,128)} %constant.105) | copy-start | bytes 300004
where the time goes:
time: 96.2 us; the launch traced here: 95.9 us
  blocking collectives  48.4 us (50%)
  local copies, waits for them, and re-layouts  27.4 us (28%)
  matrix products  15.1 us (16%)
  starting transfers between devices  2.69 us (3%)
  other arithmetic  1.8 us (2%)
    all_to_all x1, blocking collectives, shards(): lax.all_to_all(packed, 'grp', split_axis=0, concat_axis=0, tiled=True)  48.4 us
    dot_general x4, matrix products, split_product(): jnp.einsum('efab,fbm->efam', blocks, leading, preferred_element_type=jnp....  7.76 us
    reshape x1, local copies, waits for them, and re-layouts, shards(): side = side_jac.reshape(elems, 4, nface, nface)  5.89 us
    gather x3, local copies, waits for them, and re-layouts, shards(): jnp.take_along_axis(sent, coarse_perm[:, :, None], axis=1)  5.16 us
    gather x2, local copies, waits for them, and re-layouts, shards(): plus_c = jnp.take_along_axis(plus_c, coarse_perm[:, None, :], axis=2)  5.08 us
    reshape x1, local copies, waits for them, and re-layouts, shards(): xface = xface_jac.reshape(elems, 2, nface, nface)  4.66 us
    dot_general x4, matrix products, split_product(): jnp.einsum('efab,fbm->efam', blocks, remainder, preferred_element_type=jn...  3.9 us
    dot_general x4, matrix products, galerkin(): return jnp.einsum('fac,efad->efcd', left_c, inner, precision=high)  2.78 us
  transfers between devices with their start and end apart: 1, of which 0 were waited for; matrix products, arithmetic and copies ran while one was open for 21% of the time, Pallas kernels for 0%

commit v1 on v0

v1 whole, which is shorter than its diff:
```python
import functools
import jax
import jax.numpy as jnp
import numpy as np
from jax import lax
from jax.experimental import pallas as pl
from jax.experimental.pallas import tpu as pltpu
from jax.sharding import PartitionSpec as P

NV = 5
MESH = pl.DeviceIdType.MESH
ANY = pl.ANY
F32 = jnp.float32
BF16 = jnp.bfloat16
LANE = 128
ELEMS = 12
NF = 625
FLAT = 15625
ROWS = 80
ZT = 20
FACE = NV * LANE
DIAG = 13 * LANE
TURNS = ([0, 1, 2, 3], [2, 0, 3, 1], [3, 2, 1, 0], [1, 3, 0, 2])


def gll_points(degree):
    if degree == 1:
        return np.array([-1.0, 1.0])
    if degree == 2:
        return np.array([-1.0, 0.0, 1.0])
    inner_pt = np.sqrt(3.0 / 7.0)
    return np.array([-1.0, -inner_pt, 0.0, inner_pt, 1.0])


def lagrange(source_deg, target_deg):
    source = gll_points(source_deg)
    target = gll_points(target_deg)
    result = np.ones((target_deg + 1, source_deg + 1))
    for j in range(source_deg + 1):
        for m in range(source_deg + 1):
            if m != j:
                result[:, j] = result[:, j] * (target - source[m]) / (source[j] - source[m])
    return result


def split(table):
    lead = table.astype(BF16).astype(np.float64)
    return lead, (table - lead).astype(BF16).astype(np.float64)


def tables():
    line = lagrange(2, 4) @ lagrange(1, 2)
    face = np.kron(line, line)
    wide = np.kron(np.eye(32), face)
    wb = np.zeros((992, 256))
    for part, table in enumerate(split(wide)):
        wb[96:896, part * LANE:(part + 1) * LANE] = table
    w2 = np.zeros((NV, 640, 256))
    for v in range(NV):
        off = (500 * v) % LANE
        for part, table in enumerate(split(np.kron(face, np.eye(20)))):
            w2[v, off:off + 500, part * LANE:part * LANE + 80] = table
    turn = np.zeros((LANE, 6 * LANE))
    for o in (1, 2, 3):
        for jj in range(4):
            for v in range(NV):
                for kk in range(4):
                    lane = jj * 20 + v * 4 + kk
                    turn[jj * 20 + v * 4 + TURNS[o][kk], (o - 1) * LANE + lane] = 1
                    turn[TURNS[o][jj] * 20 + v * 4 + kk, (o + 2) * LANE + lane] = 1
    cube = np.kron(np.eye(NV), np.kron(np.kron(line, line), line))
    right = np.zeros((3, NF, 256))
    lead, rest = split(cube)
    for m in range(3):
        right[m, :, 40 * m:40 * m + 40] = lead
        right[m, :, LANE + 40 * m:LANE + 40 * m + 40] = rest
    left = np.concatenate([lead.T, rest.T], axis=0)
    return [jnp.asarray(t.astype(BF16)) for t in (wb, w2, turn, right, left)]


def dot(a, b):
    return jnp.dot(a, b, preferred_element_type=F32)


def halves(value):
    lead = value.astype(BF16)
    return lead, (value - lead.astype(F32)).astype(BF16)


def iota(shape, dim):
    return lax.broadcasted_iota(jnp.int32, shape, dim)


def face_rows(x_ref, s_ref, wb_ref, w2_ref, xs, zz):
    xs[0:24, 0:FLAT] = x_ref[...].reshape(24, FLAT)
    xs[32:80, 0:FLAT] = s_ref[...].reshape(48, FLAT)
    xs[24:32, :] = jnp.zeros((8, xs.shape[1]), BF16)
    xs[:, FLAT:] = jnp.zeros((ROWS, xs.shape[1] - FLAT), BF16)
    for q in range(4):
        tiles = range(q, ZT, 4)
        starts = [(800 * j) // LANE * LANE for j in tiles]
        rows = jnp.concatenate([xs[:, s:s + 896] for s in starts], axis=0)
        prod = dot(rows, wb_ref[96 - 32 * q:992 - 32 * q, :])
        both = prod[:, :LANE] + prod[:, LANE:]
        for i, j in enumerate(tiles):
            lead, rest = halves(both[ROWS * i:ROWS * (i + 1)])
            zz[0:ROWS, LANE * j:LANE * (j + 1)] = lead
            zz[ROWS:2 * ROWS, LANE * j:LANE * (j + 1)] = rest
    out = []
    for v in range(NV):
        start = (500 * v) // LANE * LANE
        prod = dot(zz[:, start:start + 640], w2_ref[v])
        out.append(prod[:ROWS, :LANE] + prod[:ROWS, LANE:] + prod[ROWS:, :LANE])
    return out


def turned(out, turn_ref, orient_ref):
    x = jnp.concatenate([t[0:32].astype(BF16) for t in out], axis=0)
    prod = dot(x, turn_ref[...])
    row = lax.rem(iota((NV * 32, LANE), 0), 32)
    o = jnp.zeros((NV * 32, LANE), jnp.int32)
    for e in range(ELEMS):
        o = jnp.where(row // 2 == e, orient_ref[e], o)
    odd = lax.rem(row, 2)
    result = x.astype(F32)
    for k in (1, 2, 3):
        result = jnp.where((o == k) & (odd == 0), prod[:, (k - 1) * LANE:k * LANE], result)
        result = jnp.where((o == k) & (odd == 1), prod[:, (k + 2) * LANE:(k + 3) * LANE], result)
    result = result.astype(BF16)
    return jnp.concatenate([result[32 * v:32 * v + 32] for v in range(NV)], axis=1)


def placement(owner_ref):
    lane = iota((16, LANE), 1)
    sub = iota((16, LANE), 0)
    on_lane = jnp.full((16, LANE), -1, jnp.int32)
    on_sub = jnp.full((16, LANE), -2, jnp.int32)
    for e in range(ELEMS):
        on_lane = jnp.where(lane == e, owner_ref[e], on_lane)
        on_sub = jnp.where(sub == e, owner_ref[e], on_sub)
    same = jnp.where((on_lane == on_sub) & (sub < lane), 1, 0)
    rank = jnp.sum(same, axis=0, keepdims=True)
    dest = jnp.where(lane < ELEMS, 2 * on_lane + rank, -1)
    return jnp.where(dest == sub, 1.0, 0.0).astype(F32)


def diag_triple(t, dv, right_ref, left_ref, hs, gs):
    for r in range(0, NF, 320):
        n = min(320, NF - r)
        prod = dot(dv[3 * t, r:r + n, :], right_ref[0])
        for m in (1, 2):
            prod += dot(dv[3 * t + m, r:r + n, :], right_ref[m])
        hs[r:r + n, :LANE], hs[r:r + n, LANE:] = halves(prod[:, :LANE] + prod[:, LANE:])
    prod = dot(left_ref[...], hs[...])
    g = prod[0:40, :LANE] + prod[0:40, LANE:] + prod[40:80, :LANE]
    for m in range(3):
        e = 3 * t + m
        gs[40 * e:40 * e + 40, :] = g if m == 0 else pltpu.roll(g, LANE - 40 * m, 1)


def diag_rows(gs):
    lane = iota((ELEMS, LANE), 1)
    tiles = [jnp.zeros((ELEMS, LANE), F32) for _ in range(13)]
    for c in range(40):
        row = gs[pl.ds(c, ELEMS, stride=40), :]
        at, shift = divmod(40 * c, LANE)
        if shift:
            row = pltpu.roll(row, shift, 1)
        tiles[at] = jnp.where((lane >= shift) & (lane < shift + 40), row, tiles[at])
        if shift + 40 > LANE:
            tiles[at + 1] = jnp.where(lane < shift + 40 - LANE, row, tiles[at + 1])
    return jnp.concatenate(tiles, axis=1)
GRP = 32
OWNERS = 8
SLOTS = 64
FIRST = 5 * FACE
LAST = FACE + DIAG


def project_and_send(orient_ref, owner_ref, x_hbm, s_hbm, d_hbm, wb_hbm, w2_hbm, tu_hbm, ri_hbm, le_hbm,
                     first_out, last_out,
                     xv, sv, dv, wb, w2, tu, ri, le, xs, zz, hs, gs, sent, minus, first, last,
                     sem, own_sem, step_send, step_recv, first_send, first_recv, last_send, last_recv):
    slab, grp = lax.axis_index("slab"), lax.axis_index("grp")
    slabs = lax.axis_size("slab")
    after, before = lax.rem(slab + 1, slabs), lax.rem(slab + slabs - 1, slabs)
    is_owner = grp < OWNERS

    pairs = [(x_hbm, xv), (s_hbm, sv), (wb_hbm, wb), (w2_hbm, w2), (tu_hbm, tu), (ri_hbm, ri), (le_hbm, le)]
    copies = [pltpu.make_async_copy(a, b, sem.at[i]) for i, (a, b) in enumerate(pairs)]
    copies += [pltpu.make_async_copy(d_hbm.at[e], dv.at[e], sem.at[7 + e]) for e in range(ELEMS)]
    for c in copies:
        c.start()

    barrier = pltpu.get_barrier_semaphore()
    pl.semaphore_signal(barrier, inc=1, device_id=(before, grp), device_id_type=MESH)

    @pl.when(is_owner)
    def _():
        def greet(i, carry):
            @pl.when(i != grp)
            def _():
                pl.semaphore_signal(barrier, inc=1, device_id=(slab, i), device_id_type=MESH)
            return carry
        lax.fori_loop(0, GRP, greet, 0)

    def to_owner(src, dst, send, recv, o):
        return pltpu.make_async_remote_copy(
            src_ref=src.at[o], dst_ref=dst.at[grp], send_sem=send.at[o], recv_sem=recv.at[grp],
            device_id=(slab, o), device_id_type=MESH)

    def keep(src, dst, i):
        return pltpu.make_async_copy(src.at[lax.rem(grp, OWNERS)], dst.at[grp], own_sem.at[i])

    def scatter(src, dst, send, recv, i):
        for k in range(OWNERS):
            o = lax.rem(grp + k, OWNERS)

            @pl.when(o != grp)
            def _():
                to_owner(src, dst, send, recv, o).start()

            @pl.when(o == grp)
            def _():
                keep(src, dst, i).start()

    def settle(src, dst, send, recv, i):
        for k in range(OWNERS):
            o = lax.rem(grp + k, OWNERS)

            @pl.when(o != grp)
            def _():
                to_owner(src, dst, send, recv, o).wait_send()

            @pl.when(o == grp)
            def _():
                keep(src, dst, i).wait()

        @pl.when(is_owner)
        def _():
            def arrive(i, carry):
                @pl.when(i != grp)
                def _():
                    pltpu.make_async_remote_copy(
                        src_ref=src.at[0], dst_ref=dst.at[i], send_sem=send.at[0], recv_sem=recv.at[i],
                        device_id=(slab, grp), device_id_type=MESH).wait_recv()
                return carry
            lax.fori_loop(0, GRP, arrive, 0)

    place = placement(owner_ref)
    pb = place.astype(BF16)
    for c in copies[:4]:
        c.wait()
    out = face_rows(xv, sv, wb, w2, xs, zz)
    copies[4].wait()
    x_rows = turned(out, tu, orient_ref)
    pick = jnp.where((iota((16, 32), 1) == 2 * iota((16, 32), 0) + 1) & (iota((16, 32), 0) < ELEMS), 1.0, 0.0)
    sent[...] = dot(pick.astype(BF16), x_rows).astype(BF16)

    @pl.when(is_owner)
    def _():
        pl.semaphore_wait(barrier, OWNERS)

    @pl.when(jnp.logical_not(is_owner))
    def _():
        pl.semaphore_wait(barrier, OWNERS + 1)

    step = pltpu.make_async_remote_copy(
        src_ref=sent, dst_ref=minus, send_sem=step_send, recv_sem=step_recv,
        device_id=(after, grp), device_id_type=MESH)
    step.start()

    side_rows = jnp.concatenate([t[32:80].astype(BF16) for t in out], axis=1)
    all_rows = jnp.concatenate([x_rows, side_rows], axis=0)
    rr, ee = iota((LANE, ROWS), 1), iota((LANE, ROWS), 0)
    picks = [jnp.where((rr == 2 * ee) & (ee < ELEMS), 1.0, 0.0)]
    picks += [jnp.where((rr == 32 + 4 * ee + f) & (ee < ELEMS), 1.0, 0.0) for f in range(4)]
    who = jnp.concatenate([dot(pb, p.astype(BF16)) for p in picks], axis=0).astype(BF16)
    placed = dot(who, all_rows).astype(BF16)
    for k in range(5):
        first[:, :, FACE * k:FACE * (k + 1)] = placed[16 * k:16 * k + 16].reshape(OWNERS, 2, FACE)
    scatter(first, first_out, first_send, first_recv, 0)

    copies[5].wait()
    copies[6].wait()
    for t in range(4):
        for m in range(3):
            copies[7 + 3 * t + m].wait()
        diag_triple(t, dv, ri, le, hs, gs)
    step.wait()
    last[:, :, :FACE] = dot(pb[:, :16], minus[...]).astype(BF16).reshape(OWNERS, 2, FACE)
    rows = diag_rows(gs).astype(BF16)
    last[:, :, FACE:] = dot(pb[:, :ELEMS], rows).astype(BF16).reshape(OWNERS, 2, DIAG)
    scatter(last, last_out, last_send, last_recv, 1)
    settle(first, first_out, first_send, first_recv, 0)
    settle(last, last_out, last_send, last_recv, 1)


def expand_tables():
    sel = [[4 * h + a for a in range(4)] for h in (0, 1)]
    sel += [[4 * a + 2 * h + b for a in (0, 1) for b in (0, 1)] for h in (0, 1)]
    sel += [[4 * a + 2 * b + h for a in (0, 1) for b in (0, 1)] for h in (0, 1)]
    ends = ((0, 1), (1, 0), (2, 3), (3, 2), (4, 5), (5, 4))
    idx = np.full((8, 8, LANE), -1, np.int32)
    for k, (a, b) in enumerate(ends):
        for u in range(5):
            for n in range(LANE):
                c, d = divmod((LANE * u + n) % 320, 40)
                if c in sel[a] and d % 8 in sel[b]:
                    idx[k, u, n] = sel[a].index(c) * 20 + d // 8 * 4 + sel[b].index(d % 8)
    return jnp.asarray(idx.reshape(64, LANE))


def expand(first_ref, last_ref, idx_ref, out_hbm, ov, sem):
    slots = SLOTS
    owner = lax.axis_index("grp") < OWNERS
    copies = [pltpu.make_async_copy(ov.at[k], out_hbm.at[k], sem.at[k]) for k in range(7)]

    @pl.when(jnp.logical_not(owner))
    def _():
        for k in range(7):
            ov[k] = jnp.zeros((slots, 1600), BF16)
            copies[k].start()

    @pl.when(owner)
    def _():
        lane = iota((slots, LANE), 1)
        ov[0] = last_ref[:, :, FACE:].reshape(slots, DIAG)[:, :1600]
        copies[0].start()
        for k in range(6):
            src = last_ref[:, :, :FACE] if k == 0 else first_ref[:, :, FACE * (k - 1):FACE * k]
            vals = src.reshape(slots, FACE).astype(F32)
            tiles = [vals[:, LANE * v:LANE * (v + 1)] for v in range(NV)]
            for u in range(5):
                idx = jnp.broadcast_to(idx_ref[8 * k + u:8 * k + u + 1, :], (slots, LANE))
                take = jnp.maximum(idx, 0)
                for p in range(3):
                    if p == 2 and u > 2:
                        continue
                    got = [jnp.take_along_axis(tiles[v], take, axis=1, mode="promise_in_bounds")
                           for v in ([2 * p] if u < 2 or p == 2 else [2 * p + 1] if u > 2 else [2 * p, 2 * p + 1])]
                    val = got[0] if len(got) == 1 else jnp.where(lane < 64, got[0], got[1])
                    val = jnp.where(idx >= 0, val, 0.0).astype(BF16)
                    at = 640 * p + LANE * u
                    width = 64 if p == 2 and u == 2 else LANE
                    ov[k + 1, :, at:at + width] = val[:, :width]
            copies[k + 1].start()

    for c in copies:
        c.wait()


def call_k3(first, last):
    vm = pl.BlockSpec(memory_space=pltpu.VMEM)
    return pl.pallas_call(
        expand,
        out_shape=jax.ShapeDtypeStruct((7, 64, 1600), BF16),
        in_specs=[vm] * 3,
        out_specs=pl.BlockSpec(memory_space=ANY),
        scratch_shapes=[pltpu.VMEM((7, 64, 1600), BF16), pltpu.SemaphoreType.DMA((7,))],
        name="expand",
    )(first, last, expand_tables())


def shards(diag_jac, xface_jac, side_jac, orient, owner):
    tabs = tables()
    smem = pl.BlockSpec(memory_space=pltpu.SMEM)
    anys = pl.BlockSpec(memory_space=ANY)
    sds = jax.ShapeDtypeStruct
    dma = pltpu.SemaphoreType.DMA
    first, last = pl.pallas_call(
        project_and_send,
        out_shape=(sds((GRP, 2, FIRST), BF16), sds((GRP, 2, LAST), BF16)),
        in_specs=[smem, smem] + [anys] * 8,
        out_specs=(anys, anys),
        scratch_shapes=[pltpu.VMEM((ELEMS, 2, FLAT), BF16), pltpu.VMEM((ELEMS, 4, FLAT), BF16),
                        pltpu.VMEM((ELEMS, NF, NF), BF16)]
        + [pltpu.VMEM(t.shape, BF16) for t in tabs]
        + [pltpu.VMEM((ROWS, 16000), BF16), pltpu.VMEM((2 * ROWS, ZT * LANE), BF16),
           pltpu.VMEM((NF, 2 * LANE), BF16), pltpu.VMEM((480, LANE), F32),
           pltpu.VMEM((16, FACE), BF16), pltpu.VMEM((16, FACE), BF16),
           pltpu.VMEM((OWNERS, 2, FIRST), BF16), pltpu.VMEM((OWNERS, 2, LAST), BF16),
           dma((19,)), dma((2,)), dma, dma, dma((OWNERS,)), dma((GRP,)), dma((OWNERS,)), dma((GRP,))],
        compiler_params=pltpu.CompilerParams(collective_id=0, has_side_effects=True),
        name="project_and_send",
    )(orient, owner, xface_jac, side_jac, diag_jac, *tabs)
    planes = call_k3(first, last)
    return jnp.transpose(planes, (1, 0, 2))


def solution(mesh):
    split_all = P(("slab", "grp"), None, None)
    vector = P(("slab", "grp"))
    return jax.shard_map(shards, mesh=mesh, in_specs=(split_all, split_all, split_all, vector, vector),
                         out_specs=split_all, check_vma=False)
```

time: 96.2 us -> 25.8 us (0.27)
  blocking collectives: 48.4 us -> 0 us
  local copies, waits for them, and re-layouts: 27.4 us -> 0 us
  Pallas kernels: 0 us -> 25.7 us
  matrix products: 15.1 us -> 0 us
  starting transfers between devices: 2.69 us -> 0 us
  other arithmetic: 1.8 us -> 0 us
    all_to_all x1 -> x0, blocking collectives: 48.4 us -> none  [shards(): lax.all_to_all(packed, 'grp', split_axis=0, concat_axis=0, tiled=True)]
    pallas_call x0 -> x2, Pallas kernels: none -> 25.7 us  [the longest x1 23.2 us: shards(): pl.pallas_call(project_and_send, out_shape=(sds((GRP, 2, FIRST), BF16), s...]
    dot_general x13 -> x0, matrix products: 15.1 us -> none  [the longest x4 7.76 us: split_product(): jnp.einsum('efab,fbm->efam', blocks, leading, preferred_element_type=jnp....]
    reshape x5 -> x0, local copies, waits for them, and re-layouts: 14.2 us -> none  [the longest x1 5.89 us: shards(): side = side_jac.reshape(elems, 4, nface, nface)]
    gather x5 -> x0, local copies, waits for them, and re-layouts: 10.2 us -> none  [the longest x3 5.16 us: shards(): jnp.take_along_axis(sent, coarse_perm[:, :, None], axis=1)]
    ppermute x1 -> x0, starting transfers between devices: 2.69 us -> none  [shifted(): lax.ppermute(array, axis, [(i, (i + by) % devices) for i in range(devices)])]
    all_to_all x1 -> x0, local copies, waits for them, and re-layouts: 1.02 us -> none  [shards(): lax.all_to_all(packed, 'grp', split_axis=0, concat_axis=0, tiled=True)]
    reduce_sum x2 -> x0, other arithmetic: 0.96 us -> none  [the longest x1 0.78 us: shards(): coarse_perm = jnp.sum(picker[:, :, None] * coarse_turns[None], axis=1)]
  transfers between devices with their start and end apart: 1 -> 0, of which waited for: 0 -> 0; matrix products, arithmetic and copies ran while one was open for 21% -> 0% of each run, Pallas kernels for 0% -> 0%
where the time goes in v1:
time: 25.8 us; the launch traced here: 25.7 us
  Pallas kernels  25.7 us (100%)
    pallas_call x1, Pallas kernels, shards(): pl.pallas_call(project_and_send, out_shape=(sds((GRP, 2, FIRST), BF16), s...  23.2 us
    pallas_call x1, Pallas kernels, call_k3(): pl.pallas_call(expand, out_shape=jax.ShapeDtypeStruct((7, 64, 1600), BF16...  2.44 us

profile of v1, /device:TPU:1, one launch (start us, length us, event | category | flops | bytes accessed | tf_op | source)
XLA Modules:
  0.0 25.7 jit_solution(10831672944362845974)
XLA Ops:
  0.0 23.2 %project_and_send.1 = (bf16[32,2,3200]{2,1,0:T(2,128)(2,1)}, bf16[32,2,2304]{2,1,0:T(2,128)(2,1)}) custom-call(s32[12]{0:T(128)} %orient_ref.1, s32[12]{0:T(128)} %owner_ref.1, bf16[12,2,15625]{2,1,0:T(2,128)(2,1)} %x_hbm.1, bf16[12,4,15625]{2,1,0:T(4,128)(2,1)} %s_hbm.1, bf16[12,625,625]{2,1,0:T(8,128)(2,1)} %d_hbm.1, ...), custom_call_target="tpu_custom_call" | custom-call | tf_op jit(solution)/shard_map/project_and_send/pallas_call | solution.py:371
  23.2 2.4 %expand.1 = bf16[7,64,1600]{2,1,0:T(8,128)(2,1)} custom-call(bf16[32,2,3200]{2,1,0:T(2,128)(2,1)} %get-tuple-element.7.first_ref, bf16[32,2,2304]{2,1,0:T(2,128)(2,1)} %get-tuple-element.8.last_ref, s32[64,128]{1,0:T(8,128)} %constant.17.clone.idx_ref), custom_call_target="tpu_custom_call" | custom-call | tf_op jit(solution)/shard_map/expand/pallas_call | solution.py:355

commit v2 on v1

--- a/solution.py
+++ b/solution.py
@@ -18,7 +18,8 @@
 FLAT = 15625
 ROWS = 80
 ZT = 20
-FACE = NV * LANE
+TILED = NV * LANE
+FACE = 400
 DIAG = 13 * LANE
 TURNS = ([0, 1, 2, 3], [2, 0, 3, 1], [3, 2, 1, 0], [1, 3, 0, 2])
 
@@ -55,11 +56,9 @@
     wb = np.zeros((992, 256))
     for part, table in enumerate(split(wide)):
         wb[96:896, part * LANE:(part + 1) * LANE] = table
-    w2 = np.zeros((NV, 640, 256))
-    for v in range(NV):
-        off = (500 * v) % LANE
-        for part, table in enumerate(split(np.kron(face, np.eye(20)))):
-            w2[v, off:off + 500, part * LANE:part * LANE + 80] = table
+    w2 = np.zeros((512, 256))
+    for part, table in enumerate(split(np.kron(face, np.eye(20)))):
+        w2[:500, part * LANE:part * LANE + 80] = table
     turn = np.zeros((LANE, 6 * LANE))
     for o in (1, 2, 3):
         for jj in range(4):
@@ -69,11 +68,10 @@
                     turn[jj * 20 + v * 4 + TURNS[o][kk], (o - 1) * LANE + lane] = 1
                     turn[TURNS[o][jj] * 20 + v * 4 + kk, (o + 2) * LANE + lane] = 1
     cube = np.kron(np.eye(NV), np.kron(np.kron(line, line), line))
-    right = np.zeros((3, NF, 256))
     lead, rest = split(cube)
-    for m in range(3):
-        right[m, :, 40 * m:40 * m + 40] = lead
-        right[m, :, LANE + 40 * m:LANE + 40 * m + 40] = rest
+    right = np.zeros((NF, LANE))
+    right[:, :40] = lead
+    right[:, 40:80] = rest
     left = np.concatenate([lead.T, rest.T], axis=0)
     return [jnp.asarray(t.astype(BF16)) for t in (wb, w2, turn, right, left)]
 
@@ -91,7 +89,7 @@
     return lax.broadcasted_iota(jnp.int32, shape, dim)
 
 
-def face_rows(x_ref, s_ref, wb_ref, w2_ref, xs, zz):
+def face_rows(x_ref, s_ref, wb_ref, w2_copy, w2_ref, xs, zf, zz):
     xs[0:24, 0:FLAT] = x_ref[...].reshape(24, FLAT)
     xs[32:80, 0:FLAT] = s_ref[...].reshape(48, FLAT)
     xs[24:32, :] = jnp.zeros((8, xs.shape[1]), BF16)
@@ -101,17 +99,43 @@
         starts = [(800 * j) // LANE * LANE for j in tiles]
         rows = jnp.concatenate([xs[:, s:s + 896] for s in starts], axis=0)
         prod = dot(rows, wb_ref[96 - 32 * q:992 - 32 * q, :])
-        both = prod[:, :LANE] + prod[:, LANE:]
         for i, j in enumerate(tiles):
-            lead, rest = halves(both[ROWS * i:ROWS * (i + 1)])
-            zz[0:ROWS, LANE * j:LANE * (j + 1)] = lead
-            zz[ROWS:2 * ROWS, LANE * j:LANE * (j + 1)] = rest
+            part = prod[ROWS * i:ROWS * (i + 1)]
+            zf[:, LANE * j:LANE * (j + 1)] = part[:, :LANE] + part[:, LANE:]
+    lane = iota((ROWS, LANE), 1)
+    for v in range(NV):
+        first, off = divmod(500 * v, LANE)
+        parts = [zf[:, LANE * (first + i):LANE * (first + i + 1)] for i in range(5 if off else 4)]
+        if off:
+            parts = [pltpu.roll(p, LANE - off, 1) for p in parts]
+            parts = [jnp.where(lane < LANE - off, parts[i], parts[i + 1]) for i in range(4)]
+        for i in range(4):
+            lead, rest = halves(parts[i])
+            at = 2 * ROWS * v
+            zz[at:at + ROWS, LANE * i:LANE * (i + 1)] = lead
+            zz[at + ROWS:at + 2 * ROWS, LANE * i:LANE * (i + 1)] = rest
+    w2_copy.wait()
+    prod = dot(zz[...], w2_ref[...])
     out = []
     for v in range(NV):
-        start = (500 * v) // LANE * LANE
-        prod = dot(zz[:, start:start + 640], w2_ref[v])
-        out.append(prod[:ROWS, :LANE] + prod[:ROWS, LANE:] + prod[ROWS:, :LANE])
+        lead, rest = prod[2 * ROWS * v:2 * ROWS * v + ROWS], prod[2 * ROWS * v + ROWS:2 * ROWS * (v + 1)]
+        out.append(lead[:, :LANE] + lead[:, LANE:] + rest[:, :LANE])
     return out
+
+
+def packed(placed, kinds):
+    lane = iota((16, LANE), 1)
+    tiles = [None] * (-(-FACE * kinds // LANE))
+    for k in range(kinds):
+        for v in range(NV):
+            value = placed[16 * k:16 * k + 16, LANE * v:LANE * (v + 1)]
+            at, shift = divmod(FACE * k + 80 * v, LANE)
+            if shift:
+                value = pltpu.roll(value, shift, 1)
+            tiles[at] = value if shift == 0 else jnp.where(lane >= shift, value, tiles[at])
+            if shift + 80 > LANE:
+                tiles[at + 1] = value
+    return jnp.concatenate(tiles, axis=1)
 
 
 def turned(out, turn_ref, orient_ref):
@@ -158,38 +182,52 @@
         gs[40 * e:40 * e + 40, :] = g if m == 0 else pltpu.roll(g, LANE - 40 * m, 1)
 
 
-def diag_rows(gs):
-    lane = iota((ELEMS, LANE), 1)
-    tiles = [jnp.zeros((ELEMS, LANE), F32) for _ in range(13)]
+def diag_tables(right_ref, wide):
+    base = right_ref[...].astype(F32)
+    lane = iota((NF, LANE), 1)
+    lead = jnp.where(lane < 40, base, 0.0)
+    rest = jnp.where(lane < 40, pltpu.roll(base, LANE - 40, 1), 0.0)
+    for m in range(3):
+        wide[m, :, :LANE] = (pltpu.roll(lead, 40 * m, 1) if m else lead).astype(BF16)
+        wide[m, :, LANE:] = (pltpu.roll(rest, 40 * m, 1) if m else rest).astype(BF16)
+
+
+def diag_rows(gs, first):
+    lane = iota((6, LANE), 1)
+    tiles = [jnp.zeros((6, LANE), F32) for _ in range(13)]
     for c in range(40):
-        row = gs[pl.ds(c, ELEMS, stride=40), :]
+        row = gs[pl.ds(40 * first + c, 6, stride=40), :]
         at, shift = divmod(40 * c, LANE)
         if shift:
             row = pltpu.roll(row, shift, 1)
         tiles[at] = jnp.where((lane >= shift) & (lane < shift + 40), row, tiles[at])
         if shift + 40 > LANE:
             tiles[at + 1] = jnp.where(lane < shift + 40 - LANE, row, tiles[at + 1])
-    return jnp.concatenate(tiles, axis=1)
+    return jnp.concatenate(tiles, axis=1).astype(BF16)
+
+
 GRP = 32
 OWNERS = 8
 SLOTS = 64
-FIRST = 5 * FACE
-LAST = FACE + DIAG
-
-
-def project_and_send(orient_ref, owner_ref, x_hbm, s_hbm, d_hbm, wb_hbm, w2_hbm, tu_hbm, ri_hbm, le_hbm,
-                     first_out, last_out,
-                     xv, sv, dv, wb, w2, tu, ri, le, xs, zz, hs, gs, sent, minus, first, last,
-                     sem, own_sem, step_send, step_recv, first_send, first_recv, last_send, last_recv):
+FIRST = 2048
+MIDDLE = 512
+
+
+def project_and_send(orient_hbm, owner_hbm, x_hbm, s_hbm, d_hbm, wb_hbm, w2_hbm, tu_hbm, ri_hbm, le_hbm,
+                     first_out, middle_out, last_out,
+                     orient_ref, owner_ref, xv, sv, dv, wb, w2, tu, ri, le, wide, xs, zf, zz, hs, gs, half, sent, minus,
+                     first, middle, last, sem, own_sem, step_send, step_recv,
+                     first_send, first_recv, middle_send, middle_recv, last_send, last_recv):
     slab, grp = lax.axis_index("slab"), lax.axis_index("grp")
     slabs = lax.axis_size("slab")
     after, before = lax.rem(slab + 1, slabs), lax.rem(slab + slabs - 1, slabs)
     is_owner = grp < OWNERS
 
-    pairs = [(x_hbm, xv), (s_hbm, sv), (wb_hbm, wb), (w2_hbm, w2), (tu_hbm, tu), (ri_hbm, ri), (le_hbm, le)]
+    pairs = [(ri_hbm, ri), (x_hbm, xv), (s_hbm, sv), (wb_hbm, wb), (w2_hbm, w2), (tu_hbm, tu), (le_hbm, le)]
+    scalars = [pltpu.make_async_copy(orient_hbm, orient_ref, sem.at[19]), pltpu.make_async_copy(owner_hbm, owner_ref, sem.at[20])]
     copies = [pltpu.make_async_copy(a, b, sem.at[i]) for i, (a, b) in enumerate(pairs)]
-    copies += [pltpu.make_async_copy(d_hbm.at[e], dv.at[e], sem.at[7 + e]) for e in range(ELEMS)]
-    for c in copies:
+    blocks = [pltpu.make_async_copy(d_hbm.at[e], dv.at[e], sem.at[7 + e]) for e in range(ELEMS)]
+    for c in scalars + copies:
         c.start()
 
     barrier = pltpu.get_barrier_semaphore()
@@ -247,12 +285,19 @@
                 return carry
             lax.fori_loop(0, GRP, arrive, 0)
 
+    for c in scalars:
+        c.wait()
     place = placement(owner_ref)
     pb = place.astype(BF16)
-    for c in copies[:4]:
+    pb_late = pltpu.roll(place, LANE - 6, 1).astype(BF16)
+    copies[0].wait()
+    diag_tables(ri, wide)
+    for c in copies[1:4]:
         c.wait()
-    out = face_rows(xv, sv, wb, w2, xs, zz)
-    copies[4].wait()
+    for c in blocks:
+        c.start()
+    out = face_rows(xv, sv, wb, copies[4], w2, xs, zf, zz)
+    copies[5].wait()
     x_rows = turned(out, tu, orient_ref)
     pick = jnp.where((iota((16, 32), 1) == 2 * iota((16, 32), 0) + 1) & (iota((16, 32), 0) < ELEMS), 1.0, 0.0)
     sent[...] = dot(pick.astype(BF16), x_rows).astype(BF16)
@@ -276,24 +321,27 @@
     picks = [jnp.where((rr == 2 * ee) & (ee < ELEMS), 1.0, 0.0)]
     picks += [jnp.where((rr == 32 + 4 * ee + f) & (ee < ELEMS), 1.0, 0.0) for f in range(4)]
     who = jnp.concatenate([dot(pb, p.astype(BF16)) for p in picks], axis=0).astype(BF16)
-    placed = dot(who, all_rows).astype(BF16)
-    for k in range(5):
-        first[:, :, FACE * k:FACE * (k + 1)] = placed[16 * k:16 * k + 16].reshape(OWNERS, 2, FACE)
+    first[...] = packed(dot(who, all_rows), 5).astype(BF16).reshape(OWNERS, 2, FIRST)
     scatter(first, first_out, first_send, first_recv, 0)
 
-    copies[5].wait()
     copies[6].wait()
     for t in range(4):
         for m in range(3):
-            copies[7 + 3 * t + m].wait()
-        diag_triple(t, dv, ri, le, hs, gs)
-    step.wait()
-    last[:, :, :FACE] = dot(pb[:, :16], minus[...]).astype(BF16).reshape(OWNERS, 2, FACE)
-    rows = diag_rows(gs).astype(BF16)
-    last[:, :, FACE:] = dot(pb[:, :ELEMS], rows).astype(BF16).reshape(OWNERS, 2, DIAG)
-    scatter(last, last_out, last_send, last_recv, 1)
+            blocks[3 * t + m].wait()
+        diag_triple(t, dv, wide, le, hs, gs)
+        if t == 1:
+            half[...] = dot(pb[:, :6], diag_rows(gs, 0))
+        if t == 2:
+            step.wait()
+            placed = dot(pb[:, :16], minus[...])
+            middle[...] = packed(placed, 1).astype(BF16).reshape(OWNERS, 2, MIDDLE)
+            scatter(middle, middle_out, middle_send, middle_recv, 1)
+    placed = half[...] + dot(pb_late[:, :6], diag_rows(gs, 6))
+    last[...] = placed.astype(BF16).reshape(OWNERS, 2, DIAG)
+    scatter(last, last_out, last_send, last_recv, 2)
     settle(first, first_out, first_send, first_recv, 0)
-    settle(last, last_out, last_send, last_recv, 1)
+    settle(middle, middle_out, middle_send, middle_recv, 1)
+    settle(last, last_out, last_send, last_recv, 2)
 
 
 def expand_tables():
@@ -301,90 +349,94 @@
     sel += [[4 * a + 2 * h + b for a in (0, 1) for b in (0, 1)] for h in (0, 1)]
     sel += [[4 * a + 2 * b + h for a in (0, 1) for b in (0, 1)] for h in (0, 1)]
     ends = ((0, 1), (1, 0), (2, 3), (3, 2), (4, 5), (5, 4))
-    idx = np.full((8, 8, LANE), -1, np.int32)
+    rows, plan = [], []
     for k, (a, b) in enumerate(ends):
-        for u in range(5):
-            for n in range(LANE):
-                c, d = divmod((LANE * u + n) % 320, 40)
-                if c in sel[a] and d % 8 in sel[b]:
-                    idx[k, u, n] = sel[a].index(c) * 20 + d // 8 * 4 + sel[b].index(d % 8)
-    return jnp.asarray(idx.reshape(64, LANE))
-
-
-def expand(first_ref, last_ref, idx_ref, out_hbm, ov, sem):
-    slots = SLOTS
+        source = np.full(13 * LANE, -1)
+        for n in range(1600):
+            c, d = divmod(n, 40)
+            if c % 8 in sel[a] and d % 8 in sel[b]:
+                source[n] = (FACE * max(k - 1, 0) + c // 8 * 80 + sel[a].index(c % 8) * 20
+                             + d // 8 * 4 + sel[b].index(d % 8))
+        for u in range(13):
+            part = source[LANE * u:LANE * (u + 1)]
+            for tile in sorted(set(part[part >= 0] // LANE)):
+                plan.append((k, u, int(tile), len(rows)))
+                rows.append(np.where(part // LANE == tile, part % LANE, -1))
+    rows += [np.full(LANE, -1)] * (-len(rows) % 8)
+    return plan, jnp.asarray(np.stack(rows).astype(np.int32))
+
+
+def expand(plan, first_ref, middle_ref, last_ref, idx_ref, out_hbm, ov, sem):
     owner = lax.axis_index("grp") < OWNERS
     copies = [pltpu.make_async_copy(ov.at[k], out_hbm.at[k], sem.at[k]) for k in range(7)]
 
     @pl.when(jnp.logical_not(owner))
     def _():
         for k in range(7):
-            ov[k] = jnp.zeros((slots, 1600), BF16)
+            ov[k] = jnp.zeros((SLOTS, 1600), BF16)
             copies[k].start()
 
     @pl.when(owner)
     def _():
-        lane = iota((slots, LANE), 1)
-        ov[0] = last_ref[:, :, FACE:].reshape(slots, DIAG)[:, :1600]
+        ov[0] = last_ref[...].reshape(SLOTS, DIAG)[:, :1600]
         copies[0].start()
+        sources = [middle_ref[...].reshape(SLOTS, MIDDLE), first_ref[...].reshape(SLOTS, FIRST)]
         for k in range(6):
-            src = last_ref[:, :, :FACE] if k == 0 else first_ref[:, :, FACE * (k - 1):FACE * k]
-            vals = src.reshape(slots, FACE).astype(F32)
-            tiles = [vals[:, LANE * v:LANE * (v + 1)] for v in range(NV)]
-            for u in range(5):
-                idx = jnp.broadcast_to(idx_ref[8 * k + u:8 * k + u + 1, :], (slots, LANE))
-                take = jnp.maximum(idx, 0)
-                for p in range(3):
-                    if p == 2 and u > 2:
-                        continue
-                    got = [jnp.take_along_axis(tiles[v], take, axis=1, mode="promise_in_bounds")
-                           for v in ([2 * p] if u < 2 or p == 2 else [2 * p + 1] if u > 2 else [2 * p, 2 * p + 1])]
-                    val = got[0] if len(got) == 1 else jnp.where(lane < 64, got[0], got[1])
-                    val = jnp.where(idx >= 0, val, 0.0).astype(BF16)
-                    at = 640 * p + LANE * u
-                    width = 64 if p == 2 and u == 2 else LANE
-                    ov[k + 1, :, at:at + width] = val[:, :width]
+            source = sources[min(k, 1)]
+            for u in range(13):
+                value = jnp.zeros((SLOTS, LANE), F32)
+                for _, _, tile, row in [p for p in plan if p[:2] == (k, u)]:
+                    idx = jnp.broadcast_to(idx_ref[row:row + 1, :], (SLOTS, LANE))
+                    part = source[:, LANE * tile:LANE * (tile + 1)].astype(F32)
+                    got = jnp.take_along_axis(part, jnp.maximum(idx, 0), axis=1, mode="promise_in_bounds")
+                    value = jnp.where(idx >= 0, got, value)
+                width = min(LANE, 1600 - LANE * u)
+                ov[k + 1, :, LANE * u:LANE * u + width] = value.astype(BF16)[:, :width]
             copies[k + 1].start()
 
     for c in copies:
         c.wait()
 
 
-def call_k3(first, last):
+def call_expand(first, middle, last):
     vm = pl.BlockSpec(memory_space=pltpu.VMEM)
+    plan, idx = expand_tables()
     return pl.pallas_call(
-        expand,
-        out_shape=jax.ShapeDtypeStruct((7, 64, 1600), BF16),
-        in_specs=[vm] * 3,
+        functools.partial(expand, plan),
+        out_shape=jax.ShapeDtypeStruct((7, SLOTS, 1600), BF16),
+        in_specs=[vm] * 4,
         out_specs=pl.BlockSpec(memory_space=ANY),
-        scratch_shapes=[pltpu.VMEM((7, 64, 1600), BF16), pltpu.SemaphoreType.DMA((7,))],
+        scratch_shapes=[pltpu.VMEM((7, SLOTS, 1600), BF16), pltpu.SemaphoreType.DMA((7,))],
+        compiler_params=pltpu.CompilerParams(vmem_limit_bytes=16 << 20),
         name="expand",
-    )(first, last, expand_tables())
+    )(first, middle, last, idx)
 
 
 def shards(diag_jac, xface_jac, side_jac, orient, owner):
     tabs = tables()
-    smem = pl.BlockSpec(memory_space=pltpu.SMEM)
     anys = pl.BlockSpec(memory_space=ANY)
     sds = jax.ShapeDtypeStruct
     dma = pltpu.SemaphoreType.DMA
-    first, last = pl.pallas_call(
+    pieces = pl.pallas_call(
         project_and_send,
-        out_shape=(sds((GRP, 2, FIRST), BF16), sds((GRP, 2, LAST), BF16)),
-        in_specs=[smem, smem] + [anys] * 8,
-        out_specs=(anys, anys),
-        scratch_shapes=[pltpu.VMEM((ELEMS, 2, FLAT), BF16), pltpu.VMEM((ELEMS, 4, FLAT), BF16),
+        out_shape=(sds((GRP, 2, FIRST), BF16), sds((GRP, 2, MIDDLE), BF16), sds((GRP, 2, DIAG), BF16)),
+        in_specs=[pl.BlockSpec(memory_space=pltpu.HBM)] * 10,
+        out_specs=(anys, anys, anys),
+        scratch_shapes=[pltpu.SMEM((ELEMS,), jnp.int32), pltpu.SMEM((ELEMS,), jnp.int32),
+                        pltpu.VMEM((ELEMS, 2, FLAT), BF16), pltpu.VMEM((ELEMS, 4, FLAT), BF16),
                         pltpu.VMEM((ELEMS, NF, NF), BF16)]
         + [pltpu.VMEM(t.shape, BF16) for t in tabs]
-        + [pltpu.VMEM((ROWS, 16000), BF16), pltpu.VMEM((2 * ROWS, ZT * LANE), BF16),
-           pltpu.VMEM((NF, 2 * LANE), BF16), pltpu.VMEM((480, LANE), F32),
-           pltpu.VMEM((16, FACE), BF16), pltpu.VMEM((16, FACE), BF16),
-           pltpu.VMEM((OWNERS, 2, FIRST), BF16), pltpu.VMEM((OWNERS, 2, LAST), BF16),
-           dma((19,)), dma((2,)), dma, dma, dma((OWNERS,)), dma((GRP,)), dma((OWNERS,)), dma((GRP,))],
-        compiler_params=pltpu.CompilerParams(collective_id=0, has_side_effects=True),
+        + [pltpu.VMEM((3, NF, 2 * LANE), BF16), pltpu.VMEM((ROWS, 16000), BF16), pltpu.VMEM((ROWS, ZT * LANE), F32),
+           pltpu.VMEM((NV * 2 * ROWS, 512), BF16), pltpu.VMEM((NF, 2 * LANE), BF16), pltpu.VMEM((480, LANE), F32),
+           pltpu.VMEM((16, DIAG), F32), pltpu.VMEM((16, TILED), BF16), pltpu.VMEM((16, TILED), BF16),
+           pltpu.VMEM((OWNERS, 2, FIRST), BF16), pltpu.VMEM((OWNERS, 2, MIDDLE), BF16), pltpu.VMEM((OWNERS, 2, DIAG), BF16),
+           dma((21,)), dma((3,)), dma, dma, dma((OWNERS,)), dma((GRP,)), dma((OWNERS,)), dma((GRP,)),
+           dma((OWNERS,)), dma((GRP,))],
+        compiler_params=pltpu.CompilerParams(collective_id=0, has_side_effects=True, vmem_limit_bytes=40 << 20),
         name="project_and_send",
-    )(orient, owner, xface_jac, side_jac, diag_jac, *tabs)
-    planes = call_k3(first, last)
+    )(*[pltpu.with_memory_space_constraint(a, pltpu.HBM)
+        for a in (orient, owner, xface_jac, side_jac, diag_jac, *tabs)])
+    planes = call_expand(*pieces)
     return jnp.transpose(planes, (1, 0, 2))
 
 

time: 25.8 us -> 24.4 us (0.946)
  Pallas kernels: 25.7 us -> 24.3 us
    pallas_call x1, Pallas kernels: 2.44 us -> 1.47 us  [call_expand(): pl.pallas_call(functools.partial(expand, plan), out_shape=jax.ShapeDtypeS...]
    pallas_call x1, Pallas kernels: 23.2 us -> 22.8 us  [shards(): pl.pallas_call(project_and_send, out_shape=(sds((GRP, 2, FIRST), BF16), s...]
where the time goes in v2:
time: 24.4 us; the launch traced here: 24.3 us
  Pallas kernels  24.3 us (100%)
    pallas_call x1, Pallas kernels, shards(): pl.pallas_call(project_and_send, out_shape=(sds((GRP, 2, FIRST), BF16), s...  22.8 us
    pallas_call x1, Pallas kernels, call_expand(): pl.pallas_call(functools.partial(expand, plan), out_shape=jax.ShapeDtypeS...  1.47 us

profile of v2, /device:TPU:1, one launch (start us, length us, event | category | flops | bytes accessed | tf_op | source)
XLA Modules:
  0.0 24.3 jit_solution(10745782701325608817)
XLA Ops:
  0.0 0.0 copy-start
  0.0 22.8 %project_and_send.1 = (bf16[32,2,2048]{2,1,0:T(2,128)(2,1)S(1)}, bf16[32,2,512]{2,1,0:T(2,128)(2,1)S(1)}, bf16[32,2,1664]{2,1,0:T(2,128)(2,1)S(1)}) custom-call(s32[12]{0:T(128)} %orient_hbm.1, s32[12]{0:T(128)} %owner_hbm.1, bf16[12,2,15625]{2,1,0:T(2,128)(2,1)} %x_hbm.1, bf16[12,4,15625]{2,1,0:T(4,128)(2,1)} %s_hbm.1, bf16[12,625,625]{2,1,0:T(8,128)(2,1)} %d_hbm.1, ...), custom_call_target="tpu_custom_call" | custom-call | tf_op jit(solution)/shard_map/project_and_send/pallas_call | solution.py:420
  22.9 0.0 copy-done
  22.9 1.5 %expand.1 = bf16[7,64,1600]{2,1,0:T(8,128)(2,1)} custom-call(bf16[32,2,2048]{2,1,0:T(2,128)(2,1)S(1)} %get-tuple-element.8.first_ref, bf16[32,2,512]{2,1,0:T(2,128)(2,1)S(1)} %get-tuple-element.9.middle_ref, bf16[32,2,1664]{2,1,0:T(2,128)(2,1)S(1)} %get-tuple-element.10.last_ref, s32[88,128]{1,0:T(8,128)S(1)} %copy-done), custom_call_target="tpu_custom_call" | custom-call | tf_op jit(solution)/shard_map/expand/pallas_call | solution.py:404
Async XLA Ops:
  0.0 22.9 %copy-start = (s32[88,128]{1,0:T(8,128)S(1)}, s32[88,128]{1,0:T(8,128)}, u32[]{:S(2)}) copy-start(s32[88,128]{1,0:T(8,128)} %constant.17.clone.idx_ref) | copy-start | bytes 135172

commit v3 on v2

--- a/solution.py
+++ b/solution.py
@@ -69,9 +69,9 @@
                     turn[TURNS[o][jj] * 20 + v * 4 + kk, (o + 2) * LANE + lane] = 1
     cube = np.kron(np.eye(NV), np.kron(np.kron(line, line), line))
     lead, rest = split(cube)
-    right = np.zeros((NF, LANE))
+    right = np.zeros((NF, 2 * LANE))
     right[:, :40] = lead
-    right[:, 40:80] = rest
+    right[:, LANE:LANE + 40] = rest
     left = np.concatenate([lead.T, rest.T], axis=0)
     return [jnp.asarray(t.astype(BF16)) for t in (wb, w2, turn, right, left)]
 
@@ -168,28 +168,19 @@
     return jnp.where(dest == sub, 1.0, 0.0).astype(F32)
 
 
-def diag_triple(t, dv, right_ref, left_ref, hs, gs):
-    for r in range(0, NF, 320):
-        n = min(320, NF - r)
-        prod = dot(dv[3 * t, r:r + n, :], right_ref[0])
-        for m in (1, 2):
-            prod += dot(dv[3 * t + m, r:r + n, :], right_ref[m])
-        hs[r:r + n, :LANE], hs[r:r + n, LANE:] = halves(prod[:, :LANE] + prod[:, LANE:])
-    prod = dot(left_ref[...], hs[...])
-    g = prod[0:40, :LANE] + prod[0:40, LANE:] + prod[40:80, :LANE]
-    for m in range(3):
-        e = 3 * t + m
-        gs[40 * e:40 * e + 40, :] = g if m == 0 else pltpu.roll(g, LANE - 40 * m, 1)
-
-
-def diag_tables(right_ref, wide):
-    base = right_ref[...].astype(F32)
-    lane = iota((NF, LANE), 1)
-    lead = jnp.where(lane < 40, base, 0.0)
-    rest = jnp.where(lane < 40, pltpu.roll(base, LANE - 40, 1), 0.0)
-    for m in range(3):
-        wide[m, :, :LANE] = (pltpu.roll(lead, 40 * m, 1) if m else lead).astype(BF16)
-        wide[m, :, LANE:] = (pltpu.roll(rest, 40 * m, 1) if m else rest).astype(BF16)
+def diag_left(e, dv, left_ref, hs, slot, i):
+    prod = dot(left_ref[...], dv[e])
+    lead, rest = halves(prod[0:40] + prod[40:80])
+    hs[slot, 80 * i:80 * i + 40, :] = lead
+    hs[slot, 80 * i + 40:80 * i + 80, :] = rest
+
+
+def diag_right(first, count, hs, slot, right_ref, gs):
+    prod = dot(hs[slot], right_ref[...])
+    for i in range(count):
+        lead, rest = prod[80 * i:80 * i + 40], prod[80 * i + 40:80 * i + 80]
+        e = first + i
+        gs[40 * e:40 * e + 40, :] = lead[:, :LANE] + lead[:, LANE:] + rest[:, :LANE]
 
 
 def diag_rows(gs, first):
@@ -211,11 +202,12 @@
 SLOTS = 64
 FIRST = 2048
 MIDDLE = 512
+GROUP = 3
 
 
 def project_and_send(orient_hbm, owner_hbm, x_hbm, s_hbm, d_hbm, wb_hbm, w2_hbm, tu_hbm, ri_hbm, le_hbm,
                      first_out, middle_out, last_out,
-                     orient_ref, owner_ref, xv, sv, dv, wb, w2, tu, ri, le, wide, xs, zf, zz, hs, gs, half, sent, minus,
+                     orient_ref, owner_ref, xv, sv, dv, wb, w2, tu, ri, le, xs, zf, zz, hs, gs, half, sent, minus,
                      first, middle, last, sem, own_sem, step_send, step_recv,
                      first_send, first_recv, middle_send, middle_recv, last_send, last_recv):
     slab, grp = lax.axis_index("slab"), lax.axis_index("grp")
@@ -223,7 +215,7 @@
     after, before = lax.rem(slab + 1, slabs), lax.rem(slab + slabs - 1, slabs)
     is_owner = grp < OWNERS
 
-    pairs = [(ri_hbm, ri), (x_hbm, xv), (s_hbm, sv), (wb_hbm, wb), (w2_hbm, w2), (tu_hbm, tu), (le_hbm, le)]
+    pairs = [(x_hbm, xv), (s_hbm, sv), (wb_hbm, wb), (w2_hbm, w2), (tu_hbm, tu), (le_hbm, le), (ri_hbm, ri)]
     scalars = [pltpu.make_async_copy(orient_hbm, orient_ref, sem.at[19]), pltpu.make_async_copy(owner_hbm, owner_ref, sem.at[20])]
     copies = [pltpu.make_async_copy(a, b, sem.at[i]) for i, (a, b) in enumerate(pairs)]
     blocks = [pltpu.make_async_copy(d_hbm.at[e], dv.at[e], sem.at[7 + e]) for e in range(ELEMS)]
@@ -251,53 +243,44 @@
         return pltpu.make_async_copy(src.at[lax.rem(grp, OWNERS)], dst.at[grp], own_sem.at[i])
 
     def scatter(src, dst, send, recv, i):
-        for k in range(OWNERS):
-            o = lax.rem(grp + k, OWNERS)
-
-            @pl.when(o != grp)
-            def _():
-                to_owner(src, dst, send, recv, o).start()
-
-            @pl.when(o == grp)
-            def _():
-                keep(src, dst, i).start()
-
-    def settle(src, dst, send, recv, i):
-        for k in range(OWNERS):
-            o = lax.rem(grp + k, OWNERS)
-
-            @pl.when(o != grp)
-            def _():
-                to_owner(src, dst, send, recv, o).wait_send()
-
-            @pl.when(o == grp)
-            def _():
-                keep(src, dst, i).wait()
+        for k in range(1, OWNERS):
+            to_owner(src, dst, send, recv, lax.rem(grp + k, OWNERS)).start()
 
         @pl.when(is_owner)
         def _():
-            def arrive(i, carry):
-                @pl.when(i != grp)
-                def _():
-                    pltpu.make_async_remote_copy(
-                        src_ref=src.at[0], dst_ref=dst.at[i], send_sem=send.at[0], recv_sem=recv.at[i],
-                        device_id=(slab, grp), device_id_type=MESH).wait_recv()
-                return carry
-            lax.fori_loop(0, GRP, arrive, 0)
+            keep(src, dst, i).start()
+
+        @pl.when(jnp.logical_not(is_owner))
+        def _():
+            to_owner(src, dst, send, recv, lax.rem(grp, OWNERS)).start()
+
+    def settle(src, dst, send, recv, i):
+        for k in range(1, OWNERS):
+            to_owner(src, dst, send, recv, lax.rem(grp + k, OWNERS)).wait_send()
+
+        @pl.when(is_owner)
+        def _():
+            keep(src, dst, i).wait()
+            for k in range(1, GRP):
+                pltpu.make_async_remote_copy(
+                    src_ref=src.at[0], dst_ref=dst.at[lax.rem(grp + k, GRP)], send_sem=send.at[0],
+                    recv_sem=recv.at[lax.rem(grp + k, GRP)], device_id=(slab, grp), device_id_type=MESH).wait_recv()
+
+        @pl.when(jnp.logical_not(is_owner))
+        def _():
+            to_owner(src, dst, send, recv, lax.rem(grp, OWNERS)).wait_send()
 
     for c in scalars:
         c.wait()
     place = placement(owner_ref)
     pb = place.astype(BF16)
     pb_late = pltpu.roll(place, LANE - 6, 1).astype(BF16)
-    copies[0].wait()
-    diag_tables(ri, wide)
-    for c in copies[1:4]:
+    for c in copies[:3]:
         c.wait()
     for c in blocks:
         c.start()
-    out = face_rows(xv, sv, wb, copies[4], w2, xs, zf, zz)
-    copies[5].wait()
+    out = face_rows(xv, sv, wb, copies[3], w2, xs, zf, zz)
+    copies[4].wait()
     x_rows = turned(out, tu, orient_ref)
     pick = jnp.where((iota((16, 32), 1) == 2 * iota((16, 32), 0) + 1) & (iota((16, 32), 0) < ELEMS), 1.0, 0.0)
     sent[...] = dot(pick.astype(BF16), x_rows).astype(BF16)
@@ -324,14 +307,20 @@
     first[...] = packed(dot(who, all_rows), 5).astype(BF16).reshape(OWNERS, 2, FIRST)
     scatter(first, first_out, first_send, first_recv, 0)
 
+    copies[5].wait()
     copies[6].wait()
-    for t in range(4):
-        for m in range(3):
-            blocks[3 * t + m].wait()
-        diag_triple(t, dv, wide, le, hs, gs)
-        if t == 1:
+    groups = ELEMS // GROUP
+    for t in range(groups + 1):
+        if t < groups:
+            for i in range(GROUP):
+                blocks[GROUP * t + i].wait()
+            for i in range(GROUP):
+                diag_left(GROUP * t + i, dv, le, hs, t % 2, i)
+        if t > 0:
+            diag_right(GROUP * (t - 1), GROUP, hs, (t - 1) % 2, ri, gs)
+        if GROUP * t == 6:
             half[...] = dot(pb[:, :6], diag_rows(gs, 0))
-        if t == 2:
+        if t == groups - 1:
             step.wait()
             placed = dot(pb[:, :16], minus[...])
             middle[...] = packed(placed, 1).astype(BF16).reshape(OWNERS, 2, MIDDLE)
@@ -426,8 +415,8 @@
                         pltpu.VMEM((ELEMS, 2, FLAT), BF16), pltpu.VMEM((ELEMS, 4, FLAT), BF16),
                         pltpu.VMEM((ELEMS, NF, NF), BF16)]
         + [pltpu.VMEM(t.shape, BF16) for t in tabs]
-        + [pltpu.VMEM((3, NF, 2 * LANE), BF16), pltpu.VMEM((ROWS, 16000), BF16), pltpu.VMEM((ROWS, ZT * LANE), F32),
-           pltpu.VMEM((NV * 2 * ROWS, 512), BF16), pltpu.VMEM((NF, 2 * LANE), BF16), pltpu.VMEM((480, LANE), F32),
+        + [pltpu.VMEM((ROWS, 16000), BF16), pltpu.VMEM((ROWS, ZT * LANE), F32),
+           pltpu.VMEM((NV * 2 * ROWS, 512), BF16), pltpu.VMEM((2, 80 * GROUP, NF), BF16), pltpu.VMEM((480, LANE), F32),
            pltpu.VMEM((16, DIAG), F32), pltpu.VMEM((16, TILED), BF16), pltpu.VMEM((16, TILED), BF16),
            pltpu.VMEM((OWNERS, 2, FIRST), BF16), pltpu.VMEM((OWNERS, 2, MIDDLE), BF16), pltpu.VMEM((OWNERS, 2, DIAG), BF16),
            dma((21,)), dma((3,)), dma, dma, dma((OWNERS,)), dma((GRP,)), dma((OWNERS,)), dma((GRP,)),

time: 24.4 us -> 22.4 us (0.918)
  Pallas kernels: 24.3 us -> 22.3 us
    pallas_call x1, Pallas kernels: 22.8 us -> 20.8 us  [shards(): pl.pallas_call(project_and_send, out_shape=(sds((GRP, 2, FIRST), BF16), s...]
where the time goes in v3:
time: 22.4 us; the launch traced here: 22.3 us
  Pallas kernels  22.3 us (100%)
    pallas_call x1, Pallas kernels, shards(): pl.pallas_call(project_and_send, out_shape=(sds((GRP, 2, FIRST), BF16), s...  20.8 us
    pallas_call x1, Pallas kernels, call_expand(): pl.pallas_call(functools.partial(expand, plan), out_shape=jax.ShapeDtypeS...  1.47 us

profile of v3, /device:TPU:1, one launch (start us, length us, event | category | flops | bytes accessed | tf_op | source)
XLA Modules:
  0.0 22.3 jit_solution(11867490383657738806)
XLA Ops:
  0.0 0.0 copy-start
  0.0 20.8 %project_and_send.1 = (bf16[32,2,2048]{2,1,0:T(2,128)(2,1)S(1)}, bf16[32,2,512]{2,1,0:T(2,128)(2,1)S(1)}, bf16[32,2,1664]{2,1,0:T(2,128)(2,1)S(1)}) custom-call(s32[12]{0:T(128)} %orient_hbm.1, s32[12]{0:T(128)} %owner_hbm.1, bf16[12,2,15625]{2,1,0:T(2,128)(2,1)} %x_hbm.1, bf16[12,4,15625]{2,1,0:T(4,128)(2,1)} %s_hbm.1, bf16[12,625,625]{2,1,0:T(8,128)(2,1)} %d_hbm.1, ...), custom_call_target="tpu_custom_call" | custom-call | tf_op jit(solution)/shard_map/project_and_send/pallas_call | solution.py:409
  20.8 0.0 copy-done
  20.9 1.5 %expand.1 = bf16[7,64,1600]{2,1,0:T(8,128)(2,1)} custom-call(bf16[32,2,2048]{2,1,0:T(2,128)(2,1)S(1)} %get-tuple-element.8.first_ref, bf16[32,2,512]{2,1,0:T(2,128)(2,1)S(1)} %get-tuple-element.9.middle_ref, bf16[32,2,1664]{2,1,0:T(2,128)(2,1)S(1)} %get-tuple-element.10.last_ref, s32[88,128]{1,0:T(8,128)S(1)} %copy-done), custom_call_target="tpu_custom_call" | custom-call | tf_op jit(solution)/shard_map/expand/pallas_call | solution.py:393
Async XLA Ops:
  0.0 20.8 %copy-start = (s32[88,128]{1,0:T(8,128)S(1)}, s32[88,128]{1,0:T(8,128)}, u32[]{:S(2)}) copy-start(s32[88,128]{1,0:T(8,128)} %constant.17.clone.idx_ref) | copy-start | bytes 135172

commit v4 on v3

--- a/solution.py
+++ b/solution.py
@@ -205,134 +205,6 @@
 GROUP = 3
 
 
-def project_and_send(orient_hbm, owner_hbm, x_hbm, s_hbm, d_hbm, wb_hbm, w2_hbm, tu_hbm, ri_hbm, le_hbm,
-                     first_out, middle_out, last_out,
-                     orient_ref, owner_ref, xv, sv, dv, wb, w2, tu, ri, le, xs, zf, zz, hs, gs, half, sent, minus,
-                     first, middle, last, sem, own_sem, step_send, step_recv,
-                     first_send, first_recv, middle_send, middle_recv, last_send, last_recv):
-    slab, grp = lax.axis_index("slab"), lax.axis_index("grp")
-    slabs = lax.axis_size("slab")
-    after, before = lax.rem(slab + 1, slabs), lax.rem(slab + slabs - 1, slabs)
-    is_owner = grp < OWNERS
-
-    pairs = [(x_hbm, xv), (s_hbm, sv), (wb_hbm, wb), (w2_hbm, w2), (tu_hbm, tu), (le_hbm, le), (ri_hbm, ri)]
-    scalars = [pltpu.make_async_copy(orient_hbm, orient_ref, sem.at[19]), pltpu.make_async_copy(owner_hbm, owner_ref, sem.at[20])]
-    copies = [pltpu.make_async_copy(a, b, sem.at[i]) for i, (a, b) in enumerate(pairs)]
-    blocks = [pltpu.make_async_copy(d_hbm.at[e], dv.at[e], sem.at[7 + e]) for e in range(ELEMS)]
-    for c in scalars + copies:
-        c.start()
-
-    barrier = pltpu.get_barrier_semaphore()
-    pl.semaphore_signal(barrier, inc=1, device_id=(before, grp), device_id_type=MESH)
-
-    @pl.when(is_owner)
-    def _():
-        def greet(i, carry):
-            @pl.when(i != grp)
-            def _():
-                pl.semaphore_signal(barrier, inc=1, device_id=(slab, i), device_id_type=MESH)
-            return carry
-        lax.fori_loop(0, GRP, greet, 0)
-
-    def to_owner(src, dst, send, recv, o):
-        return pltpu.make_async_remote_copy(
-            src_ref=src.at[o], dst_ref=dst.at[grp], send_sem=send.at[o], recv_sem=recv.at[grp],
-            device_id=(slab, o), device_id_type=MESH)
-
-    def keep(src, dst, i):
-        return pltpu.make_async_copy(src.at[lax.rem(grp, OWNERS)], dst.at[grp], own_sem.at[i])
-
-    def scatter(src, dst, send, recv, i):
-        for k in range(1, OWNERS):
-            to_owner(src, dst, send, recv, lax.rem(grp + k, OWNERS)).start()
-
-        @pl.when(is_owner)
-        def _():
-            keep(src, dst, i).start()
-
-        @pl.when(jnp.logical_not(is_owner))
-        def _():
-            to_owner(src, dst, send, recv, lax.rem(grp, OWNERS)).start()
-
-    def settle(src, dst, send, recv, i):
-        for k in range(1, OWNERS):
-            to_owner(src, dst, send, recv, lax.rem(grp + k, OWNERS)).wait_send()
-
-        @pl.when(is_owner)
-        def _():
-            keep(src, dst, i).wait()
-            for k in range(1, GRP):
-                pltpu.make_async_remote_copy(
-                    src_ref=src.at[0], dst_ref=dst.at[lax.rem(grp + k, GRP)], send_sem=send.at[0],
-                    recv_sem=recv.at[lax.rem(grp + k, GRP)], device_id=(slab, grp), device_id_type=MESH).wait_recv()
-
-        @pl.when(jnp.logical_not(is_owner))
-        def _():
-            to_owner(src, dst, send, recv, lax.rem(grp, OWNERS)).wait_send()
-
-    for c in scalars:
-        c.wait()
-    place = placement(owner_ref)
-    pb = place.astype(BF16)
-    pb_late = pltpu.roll(place, LANE - 6, 1).astype(BF16)
-    for c in copies[:3]:
-        c.wait()
-    for c in blocks:
-        c.start()
-    out = face_rows(xv, sv, wb, copies[3], w2, xs, zf, zz)
-    copies[4].wait()
-    x_rows = turned(out, tu, orient_ref)
-    pick = jnp.where((iota((16, 32), 1) == 2 * iota((16, 32), 0) + 1) & (iota((16, 32), 0) < ELEMS), 1.0, 0.0)
-    sent[...] = dot(pick.astype(BF16), x_rows).astype(BF16)
-
-    @pl.when(is_owner)
-    def _():
-        pl.semaphore_wait(barrier, OWNERS)
-
-    @pl.when(jnp.logical_not(is_owner))
-    def _():
-        pl.semaphore_wait(barrier, OWNERS + 1)
-
-    step = pltpu.make_async_remote_copy(
-        src_ref=sent, dst_ref=minus, send_sem=step_send, recv_sem=step_recv,
-        device_id=(after, grp), device_id_type=MESH)
-    step.start()
-
-    side_rows = jnp.concatenate([t[32:80].astype(BF16) for t in out], axis=1)
-    all_rows = jnp.concatenate([x_rows, side_rows], axis=0)
-    rr, ee = iota((LANE, ROWS), 1), iota((LANE, ROWS), 0)
-    picks = [jnp.where((rr == 2 * ee) & (ee < ELEMS), 1.0, 0.0)]
-    picks += [jnp.where((rr == 32 + 4 * ee + f) & (ee < ELEMS), 1.0, 0.0) for f in range(4)]
-    who = jnp.concatenate([dot(pb, p.astype(BF16)) for p in picks], axis=0).astype(BF16)
-    first[...] = packed(dot(who, all_rows), 5).astype(BF16).reshape(OWNERS, 2, FIRST)
-    scatter(first, first_out, first_send, first_recv, 0)
-
-    copies[5].wait()
-    copies[6].wait()
-    groups = ELEMS // GROUP
-    for t in range(groups + 1):
-        if t < groups:
-            for i in range(GROUP):
-                blocks[GROUP * t + i].wait()
-            for i in range(GROUP):
-                diag_left(GROUP * t + i, dv, le, hs, t % 2, i)
-        if t > 0:
-            diag_right(GROUP * (t - 1), GROUP, hs, (t - 1) % 2, ri, gs)
-        if GROUP * t == 6:
-            half[...] = dot(pb[:, :6], diag_rows(gs, 0))
-        if t == groups - 1:
-            step.wait()
-            placed = dot(pb[:, :16], minus[...])
-            middle[...] = packed(placed, 1).astype(BF16).reshape(OWNERS, 2, MIDDLE)
-            scatter(middle, middle_out, middle_send, middle_recv, 1)
-    placed = half[...] + dot(pb_late[:, :6], diag_rows(gs, 6))
-    last[...] = placed.astype(BF16).reshape(OWNERS, 2, DIAG)
-    scatter(last, last_out, last_send, last_recv, 2)
-    settle(first, first_out, first_send, first_recv, 0)
-    settle(middle, middle_out, middle_send, middle_recv, 1)
-    settle(last, last_out, last_send, last_recv, 2)
-
-
 def expand_tables():
     sel = [[4 * h + a for a in range(4)] for h in (0, 1)]
     sel += [[4 * a + 2 * h + b for a in (0, 1) for b in (0, 1)] for h in (0, 1)]
@@ -355,13 +227,181 @@
     return plan, jnp.asarray(np.stack(rows).astype(np.int32))
 
 
-def expand(plan, first_ref, middle_ref, last_ref, idx_ref, out_hbm, ov, sem):
+def expand_block(plan, k, source, idx_ref, store):
+    for u in range(13):
+        value = jnp.zeros((SLOTS, LANE), F32)
+        for _, _, tile, row in [p for p in plan if p[:2] == (k, u)]:
+            idx = jnp.broadcast_to(idx_ref[row:row + 1, :], (SLOTS, LANE))
+            part = source[:, LANE * tile:LANE * (tile + 1)].astype(F32)
+            got = jnp.take_along_axis(part, jnp.maximum(idx, 0), axis=1, mode="promise_in_bounds")
+            value = jnp.where(idx >= 0, got, value)
+        width = min(LANE, 1600 - LANE * u)
+        store(slice(LANE * u, LANE * u + width), value.astype(BF16)[:, :width])
+
+
+def project_and_send(plan, orient_hbm, owner_hbm, x_hbm, s_hbm, d_hbm, wb_hbm, w2_hbm, tu_hbm, ri_hbm, le_hbm,
+                     idx_hbm, planes_out, middle_out, last_out,
+                     orient_ref, owner_ref, xv, sv, dv, wb, w2, tu, ri, le, xs, zf, zz, hs, gs, half, sent, minus,
+                     first, middle, last, first_out, ov, idx_ref, sem, own_sem, plane_sem, step_send, step_recv,
+                     first_send, first_recv, middle_send, middle_recv, last_send, last_recv):
+    slab, grp = lax.axis_index("slab"), lax.axis_index("grp")
+    slabs = lax.axis_size("slab")
+    after, before = lax.rem(slab + 1, slabs), lax.rem(slab + slabs - 1, slabs)
+    is_owner = grp < OWNERS
+
+    pairs = [(x_hbm, xv), (s_hbm, sv), (wb_hbm, wb), (w2_hbm, w2), (tu_hbm, tu), (le_hbm, le), (ri_hbm, ri)]
+    idx_copy = pltpu.make_async_copy(idx_hbm, idx_ref, sem.at[21])
+    scalars = [pltpu.make_async_copy(orient_hbm, orient_ref, sem.at[19]), pltpu.make_async_copy(owner_hbm, owner_ref, sem.at[20])]
+    copies = [pltpu.make_async_copy(a, b, sem.at[i]) for i, (a, b) in enumerate(pairs)]
+    blocks = [pltpu.make_async_copy(d_hbm.at[e], dv.at[e], sem.at[7 + e]) for e in range(ELEMS)]
+    for c in scalars + copies:
+        c.start()
+
+    barrier = pltpu.get_barrier_semaphore()
+    pl.semaphore_signal(barrier, inc=1, device_id=(before, grp), device_id_type=MESH)
+
+    @pl.when(is_owner)
+    def _():
+        def greet(i, carry):
+            @pl.when(i != grp)
+            def _():
+                pl.semaphore_signal(barrier, inc=1, device_id=(slab, i), device_id_type=MESH)
+            return carry
+        lax.fori_loop(0, GRP, greet, 0)
+
+    def to_owner(src, dst, send, recv, o):
+        return pltpu.make_async_remote_copy(
+            src_ref=src.at[o], dst_ref=dst.at[grp], send_sem=send.at[o], recv_sem=recv.at[grp],
+            device_id=(slab, o), device_id_type=MESH)
+
+    def keep(src, dst, i):
+        return pltpu.make_async_copy(src.at[lax.rem(grp, OWNERS)], dst.at[grp], own_sem.at[i])
+
+    def scatter(src, dst, send, recv, i):
+        for k in range(1, OWNERS):
+            to_owner(src, dst, send, recv, lax.rem(grp + k, OWNERS)).start()
+
+        @pl.when(is_owner)
+        def _():
+            keep(src, dst, i).start()
+
+        @pl.when(jnp.logical_not(is_owner))
+        def _():
+            to_owner(src, dst, send, recv, lax.rem(grp, OWNERS)).start()
+
+    def sent_all(src, dst, send, recv):
+        for k in range(1, OWNERS):
+            to_owner(src, dst, send, recv, lax.rem(grp + k, OWNERS)).wait_send()
+
+        @pl.when(jnp.logical_not(is_owner))
+        def _():
+            to_owner(src, dst, send, recv, lax.rem(grp, OWNERS)).wait_send()
+
+    def arrived(src, dst, send, recv, i):
+        keep(src, dst, i).wait()
+        for k in range(1, GRP):
+            pltpu.make_async_remote_copy(
+                src_ref=src.at[0], dst_ref=dst.at[lax.rem(grp + k, GRP)], send_sem=send.at[0],
+                recv_sem=recv.at[lax.rem(grp + k, GRP)], device_id=(slab, grp), device_id_type=MESH).wait_recv()
+
+    for c in scalars:
+        c.wait()
+    place = placement(owner_ref)
+    pb = place.astype(BF16)
+    pb_late = pltpu.roll(place, LANE - 6, 1).astype(BF16)
+    for c in copies[:3]:
+        c.wait()
+    for c in blocks + [idx_copy]:
+        c.start()
+    out = face_rows(xv, sv, wb, copies[3], w2, xs, zf, zz)
+    copies[4].wait()
+    x_rows = turned(out, tu, orient_ref)
+    pick = jnp.where((iota((16, 32), 1) == 2 * iota((16, 32), 0) + 1) & (iota((16, 32), 0) < ELEMS), 1.0, 0.0)
+    sent[...] = dot(pick.astype(BF16), x_rows).astype(BF16)
+
+    @pl.when(is_owner)
+    def _():
+        pl.semaphore_wait(barrier, OWNERS)
+
+    @pl.when(jnp.logical_not(is_owner))
+    def _():
+        pl.semaphore_wait(barrier, OWNERS + 1)
+
+    step = pltpu.make_async_remote_copy(
+        src_ref=sent, dst_ref=minus, send_sem=step_send, recv_sem=step_recv,
+        device_id=(after, grp), device_id_type=MESH)
+    step.start()
+
+    side_rows = jnp.concatenate([t[32:80].astype(BF16) for t in out], axis=1)
+    all_rows = jnp.concatenate([x_rows, side_rows], axis=0)
+    rr, ee = iota((LANE, ROWS), 1), iota((LANE, ROWS), 0)
+    picks = [jnp.where((rr == 2 * ee) & (ee < ELEMS), 1.0, 0.0)]
+    picks += [jnp.where((rr == 32 + 4 * ee + f) & (ee < ELEMS), 1.0, 0.0) for f in range(4)]
+    who = jnp.concatenate([dot(pb, p.astype(BF16)) for p in picks], axis=0).astype(BF16)
+    first[...] = packed(dot(who, all_rows), 5).astype(BF16).reshape(OWNERS, 2, FIRST)
+    scatter(first, first_out, first_send, first_recv, 0)
+
+    copies[5].wait()
+    copies[6].wait()
+    groups = ELEMS // GROUP
+    for t in range(groups + 1):
+        if t < groups:
+            for i in range(GROUP):
+                blocks[GROUP * t + i].wait()
+            for i in range(GROUP):
+                diag_left(GROUP * t + i, dv, le, hs, t % 2, i)
+        if t > 0:
+            diag_right(GROUP * (t - 1), GROUP, hs, (t - 1) % 2, ri, gs)
+        if GROUP * t == 6:
+            half[...] = dot(pb[:, :6], diag_rows(gs, 0))
+    placed = half[...] + dot(pb_late[:, :6], diag_rows(gs, 6))
+    last[...] = placed.astype(BF16).reshape(OWNERS, 2, DIAG)
+    scatter(last, last_out, last_send, last_recv, 2)
+    step.wait()
+    placed = dot(pb[:, :16], minus[...])
+    middle[...] = packed(placed, 1).astype(BF16).reshape(OWNERS, 2, MIDDLE)
+    scatter(middle, middle_out, middle_send, middle_recv, 1)
+    planes = [pltpu.make_async_copy(ov.at[k], planes_out.at[k], plane_sem.at[k]) for k in range(5)]
+    idx_copy.wait()
+
+    @pl.when(jnp.logical_not(is_owner))
+    def _():
+        for k in range(5):
+            ov[k] = jnp.zeros((SLOTS, 1600), BF16)
+            planes[k].start()
+
+    @pl.when(is_owner)
+    def _():
+        arrived(first, first_out, first_send, first_recv, 0)
+        source = first_out[...].reshape(SLOTS, FIRST)
+        for k in range(5):
+            def store(at, value, k=k):
+                ov[k, :, at] = value
+            expand_block(plan, k + 1, source, idx_ref, store)
+            planes[k].start()
+
+    sent_all(first, first_out, first_send, first_recv)
+    sent_all(middle, middle_out, middle_send, middle_recv)
+    sent_all(last, last_out, last_send, last_recv)
+    for p in planes:
+        p.wait()
+
+    @pl.when(is_owner)
+    def _():
+        arrived(middle, middle_out, middle_send, middle_recv, 1)
+        arrived(last, last_out, last_send, last_recv, 2)
+
+
+def expand(plan, planes_ref, middle_ref, last_ref, idx_ref, out_hbm, ov, sem):
     owner = lax.axis_index("grp") < OWNERS
-    copies = [pltpu.make_async_copy(ov.at[k], out_hbm.at[k], sem.at[k]) for k in range(7)]
+    copies = [pltpu.make_async_copy(ov.at[k], out_hbm.at[k], sem.at[k]) for k in range(2)]
+    copies += [pltpu.make_async_copy(planes_ref.at[k - 2], out_hbm.at[k], sem.at[k]) for k in range(2, 7)]
+    for c in copies[2:]:
+        c.start()
 
     @pl.when(jnp.logical_not(owner))
     def _():
-        for k in range(7):
+        for k in range(2):
             ov[k] = jnp.zeros((SLOTS, 1600), BF16)
             copies[k].start()
 
@@ -369,47 +409,28 @@
     def _():
         ov[0] = last_ref[...].reshape(SLOTS, DIAG)[:, :1600]
         copies[0].start()
-        sources = [middle_ref[...].reshape(SLOTS, MIDDLE), first_ref[...].reshape(SLOTS, FIRST)]
-        for k in range(6):
-            source = sources[min(k, 1)]
-            for u in range(13):
-                value = jnp.zeros((SLOTS, LANE), F32)
-                for _, _, tile, row in [p for p in plan if p[:2] == (k, u)]:
-                    idx = jnp.broadcast_to(idx_ref[row:row + 1, :], (SLOTS, LANE))
-                    part = source[:, LANE * tile:LANE * (tile + 1)].astype(F32)
-                    got = jnp.take_along_axis(part, jnp.maximum(idx, 0), axis=1, mode="promise_in_bounds")
-                    value = jnp.where(idx >= 0, got, value)
-                width = min(LANE, 1600 - LANE * u)
-                ov[k + 1, :, LANE * u:LANE * u + width] = value.astype(BF16)[:, :width]
-            copies[k + 1].start()
+
+        def store(at, value):
+            ov[1, :, at] = value
+        expand_block(plan, 0, middle_ref[...].reshape(SLOTS, MIDDLE), idx_ref, store)
+        copies[1].start()
 
     for c in copies:
         c.wait()
 
 
-def call_expand(first, middle, last):
-    vm = pl.BlockSpec(memory_space=pltpu.VMEM)
-    plan, idx = expand_tables()
-    return pl.pallas_call(
-        functools.partial(expand, plan),
-        out_shape=jax.ShapeDtypeStruct((7, SLOTS, 1600), BF16),
-        in_specs=[vm] * 4,
-        out_specs=pl.BlockSpec(memory_space=ANY),
-        scratch_shapes=[pltpu.VMEM((7, SLOTS, 1600), BF16), pltpu.SemaphoreType.DMA((7,))],
-        compiler_params=pltpu.CompilerParams(vmem_limit_bytes=16 << 20),
-        name="expand",
-    )(first, middle, last, idx)
-
-
 def shards(diag_jac, xface_jac, side_jac, orient, owner):
     tabs = tables()
+    plan, idx = expand_tables()
     anys = pl.BlockSpec(memory_space=ANY)
+    vm = pl.BlockSpec(memory_space=pltpu.VMEM)
+    hbm = pl.BlockSpec(memory_space=pltpu.HBM)
     sds = jax.ShapeDtypeStruct
     dma = pltpu.SemaphoreType.DMA
-    pieces = pl.pallas_call(
-        project_and_send,
-        out_shape=(sds((GRP, 2, FIRST), BF16), sds((GRP, 2, MIDDLE), BF16), sds((GRP, 2, DIAG), BF16)),
-        in_specs=[pl.BlockSpec(memory_space=pltpu.HBM)] * 10,
+    planes, middle, last = pl.pallas_call(
+        functools.partial(project_and_send, plan),
+        out_shape=(sds((5, SLOTS, 1600), BF16), sds((GRP, 2, MIDDLE), BF16), sds((GRP, 2, DIAG), BF16)),
+        in_specs=[hbm] * 11,
         out_specs=(anys, anys, anys),
         scratch_shapes=[pltpu.SMEM((ELEMS,), jnp.int32), pltpu.SMEM((ELEMS,), jnp.int32),
                         pltpu.VMEM((ELEMS, 2, FLAT), BF16), pltpu.VMEM((ELEMS, 4, FLAT), BF16),
@@ -419,13 +440,22 @@
            pltpu.VMEM((NV * 2 * ROWS, 512), BF16), pltpu.VMEM((2, 80 * GROUP, NF), BF16), pltpu.VMEM((480, LANE), F32),
            pltpu.VMEM((16, DIAG), F32), pltpu.VMEM((16, TILED), BF16), pltpu.VMEM((16, TILED), BF16),
            pltpu.VMEM((OWNERS, 2, FIRST), BF16), pltpu.VMEM((OWNERS, 2, MIDDLE), BF16), pltpu.VMEM((OWNERS, 2, DIAG), BF16),
-           dma((21,)), dma((3,)), dma, dma, dma((OWNERS,)), dma((GRP,)), dma((OWNERS,)), dma((GRP,)),
+           pltpu.VMEM((GRP, 2, FIRST), BF16), pltpu.VMEM((5, SLOTS, 1600), BF16), pltpu.VMEM(idx.shape, jnp.int32),
+           dma((22,)), dma((3,)), dma((5,)), dma, dma, dma((OWNERS,)), dma((GRP,)), dma((OWNERS,)), dma((GRP,)),
            dma((OWNERS,)), dma((GRP,))],
         compiler_params=pltpu.CompilerParams(collective_id=0, has_side_effects=True, vmem_limit_bytes=40 << 20),
         name="project_and_send",
     )(*[pltpu.with_memory_space_constraint(a, pltpu.HBM)
-        for a in (orient, owner, xface_jac, side_jac, diag_jac, *tabs)])
-    planes = call_expand(*pieces)
+        for a in (orient, owner, xface_jac, side_jac, diag_jac, *tabs, idx)])
+    planes = pl.pallas_call(
+        functools.partial(expand, plan),
+        out_shape=sds((7, SLOTS, 1600), BF16),
+        in_specs=[vm, vm, vm, vm],
+        out_specs=hbm,
+        scratch_shapes=[pltpu.VMEM((2, SLOTS, 1600), BF16), dma((7,))],
+        compiler_params=pltpu.CompilerParams(vmem_limit_bytes=16 << 20),
+        name="expand",
+    )(planes, middle, last, idx)
     return jnp.transpose(planes, (1, 0, 2))
 
 

time: 22.4 us -> 22 us (0.982)
  Pallas kernels: 22.3 us -> 21.9 us
    pallas_call x2, Pallas kernels: 22.3 us -> 21.9 us  [the longest x1 20.7 us: shards(): pl.pallas_call(functools.partial(project_and_send, plan), out_shape=(sds(...]
where the time goes in v4:
time: 22 us; the launch traced here: 21.9 us
  Pallas kernels  21.9 us (100%)
    pallas_call x1, Pallas kernels, shards(): pl.pallas_call(functools.partial(project_and_send, plan), out_shape=(sds(...  20.7 us
    pallas_call x1, Pallas kernels, shards(): pl.pallas_call(functools.partial(expand, plan), out_shape=sds((7, SLOTS,...  1.18 us

profile of v4, /device:TPU:1, one launch (start us, length us, event | category | flops | bytes accessed | tf_op | source)
XLA Modules:
  0.0 21.9 jit_solution(5781779893671117755)
XLA Ops:
  0.0 0.0 copy-start
  0.0 20.7 %project_and_send.1 = (bf16[5,64,1600]{2,1,0:T(8,128)(2,1)S(1)}, bf16[32,2,512]{2,1,0:T(2,128)(2,1)S(1)}, bf16[32,2,1664]{2,1,0:T(2,128)(2,1)S(1)}) custom-call(s32[12]{0:T(128)} %orient_hbm.1, s32[12]{0:T(128)} %owner_hbm.1, bf16[12,2,15625]{2,1,0:T(2,128)(2,1)} %x_hbm.1, bf16[12,4,15625]{2,1,0:T(4,128)(2,1)} %s_hbm.1, bf16[12,625,625]{2,1,0:T(8,128)(2,1)} %d_hbm.1, ...), custom_call_target="tpu_custom_call" | custom-call | tf_op jit(solution)/shard_map/project_and_send/pallas_call | solution.py:430
  20.7 0.0 copy-done
  20.7 1.2 %expand.1 = bf16[7,64,1600]{2,1,0:T(8,128)(2,1)} custom-call(bf16[5,64,1600]{2,1,0:T(8,128)(2,1)S(1)} %get-tuple-element.8.planes_ref, bf16[32,2,512]{2,1,0:T(2,128)(2,1)S(1)} %get-tuple-element.9.middle_ref, bf16[32,2,1664]{2,1,0:T(2,128)(2,1)S(1)} %get-tuple-element.10.last_ref, s32[88,128]{1,0:T(8,128)S(1)} %copy-done), custom_call_target="tpu_custom_call" | custom-call | tf_op jit(solution)/shard_map/expand/pallas_call | solution.py:450
Async XLA Ops:
  0.0 20.7 %copy-start = (s32[88,128]{1,0:T(8,128)S(1)}, s32[88,128]{1,0:T(8,128)}, u32[]{:S(2)}) copy-start(s32[88,128]{1,0:T(8,128)} %constant.17.clone.idx_hbm.idx_ref) | copy-start | bytes 135172

commit v5 on v4

--- a/solution.py
+++ b/solution.py
@@ -201,7 +201,8 @@
 OWNERS = 8
 SLOTS = 64
 FIRST = 2048
-MIDDLE = 512
+MINUS = 512
+LAST = MINUS + DIAG
 GROUP = 3
 
 
@@ -240,10 +241,10 @@
 
 
 def project_and_send(plan, orient_hbm, owner_hbm, x_hbm, s_hbm, d_hbm, wb_hbm, w2_hbm, tu_hbm, ri_hbm, le_hbm,
-                     idx_hbm, planes_out, middle_out, last_out,
+                     idx_hbm, planes_out, last_out,
                      orient_ref, owner_ref, xv, sv, dv, wb, w2, tu, ri, le, xs, zf, zz, hs, gs, half, sent, minus,
-                     first, middle, last, first_out, ov, idx_ref, sem, own_sem, plane_sem, step_send, step_recv,
-                     first_send, first_recv, middle_send, middle_recv, last_send, last_recv):
+                     first, last, first_out, ov, idx_ref, sem, own_sem, plane_sem, step_send, step_recv,
+                     first_send, first_recv, last_send, last_recv):
     slab, grp = lax.axis_index("slab"), lax.axis_index("grp")
     slabs = lax.axis_size("slab")
     after, before = lax.rem(slab + 1, slabs), lax.rem(slab + slabs - 1, slabs)
@@ -254,7 +255,7 @@
     scalars = [pltpu.make_async_copy(orient_hbm, orient_ref, sem.at[19]), pltpu.make_async_copy(owner_hbm, owner_ref, sem.at[20])]
     copies = [pltpu.make_async_copy(a, b, sem.at[i]) for i, (a, b) in enumerate(pairs)]
     blocks = [pltpu.make_async_copy(d_hbm.at[e], dv.at[e], sem.at[7 + e]) for e in range(ELEMS)]
-    for c in scalars + copies:
+    for c in scalars + copies[:4]:
         c.start()
 
     barrier = pltpu.get_barrier_semaphore()
@@ -277,9 +278,12 @@
     def keep(src, dst, i):
         return pltpu.make_async_copy(src.at[lax.rem(grp, OWNERS)], dst.at[grp], own_sem.at[i])
 
+    def nth(k):
+        return jnp.where(is_owner & (grp <= k), k + 1, k)
+
     def scatter(src, dst, send, recv, i):
-        for k in range(1, OWNERS):
-            to_owner(src, dst, send, recv, lax.rem(grp + k, OWNERS)).start()
+        for k in range(OWNERS - 1):
+            to_owner(src, dst, send, recv, nth(k)).start()
 
         @pl.when(is_owner)
         def _():
@@ -287,15 +291,15 @@
 
         @pl.when(jnp.logical_not(is_owner))
         def _():
-            to_owner(src, dst, send, recv, lax.rem(grp, OWNERS)).start()
+            to_owner(src, dst, send, recv, OWNERS - 1).start()
 
     def sent_all(src, dst, send, recv):
-        for k in range(1, OWNERS):
-            to_owner(src, dst, send, recv, lax.rem(grp + k, OWNERS)).wait_send()
+        for k in range(OWNERS - 1):
+            to_owner(src, dst, send, recv, nth(k)).wait_send()
 
         @pl.when(jnp.logical_not(is_owner))
         def _():
-            to_owner(src, dst, send, recv, lax.rem(grp, OWNERS)).wait_send()
+            to_owner(src, dst, send, recv, OWNERS - 1).wait_send()
 
     def arrived(src, dst, send, recv, i):
         keep(src, dst, i).wait()
@@ -311,7 +315,7 @@
     pb_late = pltpu.roll(place, LANE - 6, 1).astype(BF16)
     for c in copies[:3]:
         c.wait()
-    for c in blocks + [idx_copy]:
+    for c in copies[4:] + blocks + [idx_copy]:
         c.start()
     out = face_rows(xv, sv, wb, copies[3], w2, xs, zf, zz)
     copies[4].wait()
@@ -355,12 +359,11 @@
         if GROUP * t == 6:
             half[...] = dot(pb[:, :6], diag_rows(gs, 0))
     placed = half[...] + dot(pb_late[:, :6], diag_rows(gs, 6))
-    last[...] = placed.astype(BF16).reshape(OWNERS, 2, DIAG)
-    scatter(last, last_out, last_send, last_recv, 2)
+    last[:, :, MINUS:] = placed.astype(BF16).reshape(OWNERS, 2, DIAG)
     step.wait()
     placed = dot(pb[:, :16], minus[...])
-    middle[...] = packed(placed, 1).astype(BF16).reshape(OWNERS, 2, MIDDLE)
-    scatter(middle, middle_out, middle_send, middle_recv, 1)
+    last[:, :, :MINUS] = packed(placed, 1).astype(BF16).reshape(OWNERS, 2, MINUS)
+    scatter(last, last_out, last_send, last_recv, 1)
     planes = [pltpu.make_async_copy(ov.at[k], planes_out.at[k], plane_sem.at[k]) for k in range(5)]
     idx_copy.wait()
 
@@ -381,18 +384,16 @@
             planes[k].start()
 
     sent_all(first, first_out, first_send, first_recv)
-    sent_all(middle, middle_out, middle_send, middle_recv)
     sent_all(last, last_out, last_send, last_recv)
     for p in planes:
         p.wait()
 
     @pl.when(is_owner)
     def _():
-        arrived(middle, middle_out, middle_send, middle_recv, 1)
-        arrived(last, last_out, last_send, last_recv, 2)
-
-
-def expand(plan, planes_ref, middle_ref, last_ref, idx_ref, out_hbm, ov, sem):
+        arrived(last, last_out, last_send, last_recv, 1)
+
+
+def expand(plan, planes_ref, last_ref, idx_ref, out_hbm, ov, sem):
     owner = lax.axis_index("grp") < OWNERS
     copies = [pltpu.make_async_copy(ov.at[k], out_hbm.at[k], sem.at[k]) for k in range(2)]
     copies += [pltpu.make_async_copy(planes_ref.at[k - 2], out_hbm.at[k], sem.at[k]) for k in range(2, 7)]
@@ -407,12 +408,12 @@
 
     @pl.when(owner)
     def _():
-        ov[0] = last_ref[...].reshape(SLOTS, DIAG)[:, :1600]
+        ov[0] = last_ref[:, :, MINUS:].reshape(SLOTS, DIAG)[:, :1600]
         copies[0].start()
 
         def store(at, value):
             ov[1, :, at] = value
-        expand_block(plan, 0, middle_ref[...].reshape(SLOTS, MIDDLE), idx_ref, store)
+        expand_block(plan, 0, last_ref[:, :, :MINUS].reshape(SLOTS, MINUS), idx_ref, store)
         copies[1].start()
 
     for c in copies:
@@ -427,11 +428,11 @@
     hbm = pl.BlockSpec(memory_space=pltpu.HBM)
     sds = jax.ShapeDtypeStruct
     dma = pltpu.SemaphoreType.DMA
-    planes, middle, last = pl.pallas_call(
+    planes, last = pl.pallas_call(
         functools.partial(project_and_send, plan),
-        out_shape=(sds((5, SLOTS, 1600), BF16), sds((GRP, 2, MIDDLE), BF16), sds((GRP, 2, DIAG), BF16)),
+        out_shape=(sds((5, SLOTS, 1600), BF16), sds((GRP, 2, LAST), BF16)),
         in_specs=[hbm] * 11,
-        out_specs=(anys, anys, anys),
+        out_specs=(anys, anys),
         scratch_shapes=[pltpu.SMEM((ELEMS,), jnp.int32), pltpu.SMEM((ELEMS,), jnp.int32),
                         pltpu.VMEM((ELEMS, 2, FLAT), BF16), pltpu.VMEM((ELEMS, 4, FLAT), BF16),
                         pltpu.VMEM((ELEMS, NF, NF), BF16)]
@@ -439,10 +440,9 @@
         + [pltpu.VMEM((ROWS, 16000), BF16), pltpu.VMEM((ROWS, ZT * LANE), F32),
            pltpu.VMEM((NV * 2 * ROWS, 512), BF16), pltpu.VMEM((2, 80 * GROUP, NF), BF16), pltpu.VMEM((480, LANE), F32),
            pltpu.VMEM((16, DIAG), F32), pltpu.VMEM((16, TILED), BF16), pltpu.VMEM((16, TILED), BF16),
-           pltpu.VMEM((OWNERS, 2, FIRST), BF16), pltpu.VMEM((OWNERS, 2, MIDDLE), BF16), pltpu.VMEM((OWNERS, 2, DIAG), BF16),
+           pltpu.VMEM((OWNERS, 2, FIRST), BF16), pltpu.VMEM((OWNERS, 2, LAST), BF16),
            pltpu.VMEM((GRP, 2, FIRST), BF16), pltpu.VMEM((5, SLOTS, 1600), BF16), pltpu.VMEM(idx.shape, jnp.int32),
-           dma((22,)), dma((3,)), dma((5,)), dma, dma, dma((OWNERS,)), dma((GRP,)), dma((OWNERS,)), dma((GRP,)),
-           dma((OWNERS,)), dma((GRP,))],
+           dma((22,)), dma((2,)), dma((5,)), dma, dma, dma((OWNERS,)), dma((GRP,)), dma((OWNERS,)), dma((GRP,))],
         compiler_params=pltpu.CompilerParams(collective_id=0, has_side_effects=True, vmem_limit_bytes=40 << 20),
         name="project_and_send",
     )(*[pltpu.with_memory_space_constraint(a, pltpu.HBM)
@@ -450,12 +450,12 @@
     planes = pl.pallas_call(
         functools.partial(expand, plan),
         out_shape=sds((7, SLOTS, 1600), BF16),
-        in_specs=[vm, vm, vm, vm],
+        in_specs=[vm, vm, vm],
         out_specs=hbm,
         scratch_shapes=[pltpu.VMEM((2, SLOTS, 1600), BF16), dma((7,))],
         compiler_params=pltpu.CompilerParams(vmem_limit_bytes=16 << 20),
         name="expand",
-    )(planes, middle, last, idx)
+    )(planes, last, idx)
     return jnp.transpose(planes, (1, 0, 2))
 
 

time: 22 us -> 21.4 us (0.973)
  Pallas kernels: 21.9 us -> 21.3 us
    pallas_call x1, Pallas kernels: 20.7 us -> 20.1 us  [shards(): pl.pallas_call(functools.partial(project_and_send, plan), out_shape=(sds(...]
where the time goes in v5:
time: 21.4 us; the launch traced here: 21.3 us
  Pallas kernels  21.3 us (100%)
    pallas_call x1, Pallas kernels, shards(): pl.pallas_call(functools.partial(project_and_send, plan), out_shape=(sds(...  20.1 us
    pallas_call x1, Pallas kernels, shards(): pl.pallas_call(functools.partial(expand, plan), out_shape=sds((7, SLOTS,...  1.18 us

profile of v5, /device:TPU:1, one launch (start us, length us, event | category | flops | bytes accessed | tf_op | source)
XLA Modules:
  0.0 21.3 jit_solution(17607498364005799578)
XLA Ops:
  0.0 0.0 copy-start
  0.0 20.1 %project_and_send.1 = (bf16[5,64,1600]{2,1,0:T(8,128)(2,1)S(1)}, bf16[32,2,2176]{2,1,0:T(2,128)(2,1)S(1)}) custom-call(s32[12]{0:T(128)} %orient_hbm.1, s32[12]{0:T(128)} %owner_hbm.1, bf16[12,2,15625]{2,1,0:T(2,128)(2,1)} %x_hbm.1, bf16[12,4,15625]{2,1,0:T(4,128)(2,1)} %s_hbm.1, bf16[12,625,625]{2,1,0:T(8,128)(2,1)} %d_hbm.1, ...), custom_call_target="tpu_custom_call" | custom-call | tf_op jit(solution)/shard_map/project_and_send/pallas_call | solution.py:431
  20.1 0.0 copy-done
  20.1 1.2 %expand.1 = bf16[7,64,1600]{2,1,0:T(8,128)(2,1)} custom-call(bf16[5,64,1600]{2,1,0:T(8,128)(2,1)S(1)} %get-tuple-element.7.planes_ref, bf16[32,2,2176]{2,1,0:T(2,128)(2,1)S(1)} %get-tuple-element.8.last_ref, s32[88,128]{1,0:T(8,128)S(1)} %copy-done), custom_call_target="tpu_custom_call" | custom-call | tf_op jit(solution)/shard_map/expand/pallas_call | solution.py:450
Async XLA Ops:
  0.0 20.1 %copy-start = (s32[88,128]{1,0:T(8,128)S(1)}, s32[88,128]{1,0:T(8,128)}, u32[]{:S(2)}) copy-start(s32[88,128]{1,0:T(8,128)} %constant.17.clone.idx_hbm.idx_ref) | copy-start | bytes 135172

commit v6 on v5

--- a/solution.py
+++ b/solution.py
@@ -123,13 +123,13 @@
     return out
 
 
-def packed(placed, kinds):
+def packed(placed, kinds, start=0):
     lane = iota((16, LANE), 1)
-    tiles = [None] * (-(-FACE * kinds // LANE))
+    tiles = [jnp.zeros((16, LANE), F32)] * (-(-(start + FACE * kinds) // LANE))
     for k in range(kinds):
         for v in range(NV):
             value = placed[16 * k:16 * k + 16, LANE * v:LANE * (v + 1)]
-            at, shift = divmod(FACE * k + 80 * v, LANE)
+            at, shift = divmod(start + FACE * k + 80 * v, LANE)
             if shift:
                 value = pltpu.roll(value, shift, 1)
             tiles[at] = value if shift == 0 else jnp.where(lane >= shift, value, tiles[at])
@@ -202,7 +202,8 @@
 SLOTS = 64
 FIRST = 2048
 MINUS = 512
-LAST = MINUS + DIAG
+SHARED = DIAG - LANE
+LAST = SHARED + MINUS
 GROUP = 3
 
 
@@ -217,7 +218,7 @@
         for n in range(1600):
             c, d = divmod(n, 40)
             if c % 8 in sel[a] and d % 8 in sel[b]:
-                source[n] = (FACE * max(k - 1, 0) + c // 8 * 80 + sel[a].index(c % 8) * 20
+                source[n] = ((FACE * (k - 1) if k else 64) + c // 8 * 80 + sel[a].index(c % 8) * 20
                              + d // 8 * 4 + sel[b].index(d % 8))
         for u in range(13):
             part = source[LANE * u:LANE * (u + 1)]
@@ -343,7 +344,6 @@
     picks += [jnp.where((rr == 32 + 4 * ee + f) & (ee < ELEMS), 1.0, 0.0) for f in range(4)]
     who = jnp.concatenate([dot(pb, p.astype(BF16)) for p in picks], axis=0).astype(BF16)
     first[...] = packed(dot(who, all_rows), 5).astype(BF16).reshape(OWNERS, 2, FIRST)
-    scatter(first, first_out, first_send, first_recv, 0)
 
     copies[5].wait()
     copies[6].wait()
@@ -356,13 +356,16 @@
                 diag_left(GROUP * t + i, dv, le, hs, t % 2, i)
         if t > 0:
             diag_right(GROUP * (t - 1), GROUP, hs, (t - 1) % 2, ri, gs)
+        if t == 0:
+            scatter(first, first_out, first_send, first_recv, 0)
         if GROUP * t == 6:
             half[...] = dot(pb[:, :6], diag_rows(gs, 0))
     placed = half[...] + dot(pb_late[:, :6], diag_rows(gs, 6))
-    last[:, :, MINUS:] = placed.astype(BF16).reshape(OWNERS, 2, DIAG)
+    last[:, :, :SHARED] = placed[:, :SHARED].astype(BF16).reshape(OWNERS, 2, SHARED)
     step.wait()
-    placed = dot(pb[:, :16], minus[...])
-    last[:, :, :MINUS] = packed(placed, 1).astype(BF16).reshape(OWNERS, 2, MINUS)
+    tail = packed(dot(pb[:, :16], minus[...]), 1, 64)
+    tail = jnp.where(iota((16, MINUS), 1) < 64, jnp.concatenate([placed[:, SHARED:], tail[:, LANE:]], axis=1), tail)
+    last[:, :, SHARED:] = tail.astype(BF16).reshape(OWNERS, 2, MINUS)
     scatter(last, last_out, last_send, last_recv, 1)
     planes = [pltpu.make_async_copy(ov.at[k], planes_out.at[k], plane_sem.at[k]) for k in range(5)]
     idx_copy.wait()
@@ -408,12 +411,12 @@
 
     @pl.when(owner)
     def _():
-        ov[0] = last_ref[:, :, MINUS:].reshape(SLOTS, DIAG)[:, :1600]
+        ov[0] = last_ref[:, :, :DIAG].reshape(SLOTS, DIAG)[:, :1600]
         copies[0].start()
 
         def store(at, value):
             ov[1, :, at] = value
-        expand_block(plan, 0, last_ref[:, :, :MINUS].reshape(SLOTS, MINUS), idx_ref, store)
+        expand_block(plan, 0, last_ref[:, :, SHARED:].reshape(SLOTS, MINUS), idx_ref, store)
         copies[1].start()
 
     for c in copies:

time: 21.4 us -> 21.3 us (level)
  no operation moved by 1% of the time
where the time goes in v6:
time: 21.3 us; the launch traced here: 21.2 us
  Pallas kernels  21.1 us (99%)
    pallas_call x1, Pallas kernels, shards(): pl.pallas_call(functools.partial(project_and_send, plan), out_shape=(sds(...  20 us
    pallas_call x1, Pallas kernels, shards(): pl.pallas_call(functools.partial(expand, plan), out_shape=sds((7, SLOTS,...  1.18 us

profile of v6, /device:TPU:1, one launch (start us, length us, event | category | flops | bytes accessed | tf_op | source)
XLA Modules:
  0.0 21.2 jit_solution(16736489930711674453)
XLA Ops:
  0.0 0.0 copy-start
  0.0 20.0 %project_and_send.1 = (bf16[5,64,1600]{2,1,0:T(8,128)(2,1)S(1)}, bf16[32,2,2048]{2,1,0:T(2,128)(2,1)S(1)}) custom-call(s32[12]{0:T(128)} %orient_hbm.1, s32[12]{0:T(128)} %owner_hbm.1, bf16[12,2,15625]{2,1,0:T(2,128)(2,1)} %x_hbm.1, bf16[12,4,15625]{2,1,0:T(4,128)(2,1)} %s_hbm.1, bf16[12,625,625]{2,1,0:T(8,128)(2,1)} %d_hbm.1, ...), custom_call_target="tpu_custom_call" | custom-call | tf_op jit(solution)/shard_map/project_and_send/pallas_call | solution.py:434
  20.0 0.0 copy-done
  20.0 1.2 %expand.1 = bf16[7,64,1600]{2,1,0:T(8,128)(2,1)} custom-call(bf16[5,64,1600]{2,1,0:T(8,128)(2,1)S(1)} %get-tuple-element.7.planes_ref, bf16[32,2,2048]{2,1,0:T(2,128)(2,1)S(1)} %get-tuple-element.8.last_ref, s32[88,128]{1,0:T(8,128)S(1)} %copy-done), custom_call_target="tpu_custom_call" | custom-call | tf_op jit(solution)/shard_map/expand/pallas_call | solution.py:453
Async XLA Ops:
  0.0 20.0 %copy-start = (s32[88,128]{1,0:T(8,128)S(1)}, s32[88,128]{1,0:T(8,128)}, u32[]{:S(2)}) copy-start(s32[88,128]{1,0:T(8,128)} %constant.17.clone.idx_hbm.idx_ref) | copy-start | bytes 135172
